TPU v7x, 32 devices: a whole 2x2x4 slice. The times are simulated.
32 devices in a mesh: dp: 8 (over z, core), tensor: 4 (over y, x).
Axes of the slice: x: 2, y: 2, z: 4, core: 2. Of those that a mesh axis runs over, the one named last changes fastest.
Arguments:
- tokens: bfloat16 [4096, 4096], P('dp', 'tensor'), may hold values from -6 to 6
- butterfly: bfloat16 [64, 5, 256, 256], P('tensor', None, 'dp'), may hold values from -0.15625 to 0.15625
- left_factor: bfloat16 [4096, 256], P(('tensor', 'dp')), may hold values from -0.09375 to 0.09375
- right_factor: bfloat16 [256, 16384], P('dp', 'tensor'), may hold values from -0.375 to 0.375
- cotangent: bfloat16 [4096, 16384], P('dp', 'tensor'), may hold values from -6 to 6
Outputs:
- hidden: bfloat16 [4096, 16384], P('dp', 'tensor')
- grad_tokens: bfloat16 [4096, 4096], P('dp', 'tensor')
- grad_butterfly: bfloat16 [64, 5, 256, 256], P('tensor', None, 'dp')
- grad_left: bfloat16 [4096, 256], P(('tensor', 'dp'))
- grad_right: bfloat16 [256, 16384], P('dp', 'tensor')
All inputs are finite; a program needn't handle non-finite values.
Results may differ from a plain program's by a relative error of at most 0.02.
Values may be sent and summed in bfloat16 or wider, within the bound.
A program may use at most 128 MiB of HBM per device.

v0:
```python
import jax
import jax.numpy as jnp
from jax import lax
from jax.sharding import PartitionSpec as P

BLK = 256
LOG = 4


ROOT_HALF = 0.7071067811865476
INV_ROOT_TWO_PI = 0.3989422804014327


def swapped(block, axis, stride):
    count = lax.axis_size(axis)
    route = []
    for low in range(count):
        high = low | 1 << stride
        if high != low and high < count:
            route += [(low, high), (high, low)]
    return lax.ppermute(block, axis, route)


def gelu_pair(preact):
    cdf = 0.5 * (1.0 + jax.scipy.special.erf(preact * ROOT_HALF))
    return (preact * cdf, cdf + preact * INV_ROOT_TWO_PI * jnp.exp(-0.5 * preact * preact))


def flip_blocks(blocks, stride):
    full_shape = blocks.shape
    leading = full_shape[:-2]
    block_count = full_shape[-2]
    halves = blocks.reshape(leading + (block_count // (2 * stride), 2, stride, full_shape[-1]))
    return jnp.flip(halves, axis=-3).reshape(full_shape)


def per_device(tokens, butterfly, left_factor, right_factor, cotangent):
    rows_here = tokens.shape[0]
    blocks_here = tokens.shape[1] // BLK
    shift_bits = blocks_here.bit_length() - 1
    hidden_blocks = right_factor.shape[1] // BLK
    group_ratio = hidden_blocks // blocks_here
    weights, left_full, right_full = (
        lax.all_gather(butterfly, "dp", axis=2, tiled=True),
        lax.all_gather(left_factor, "dp", axis=0, tiled=True),
        lax.all_gather(right_factor, "dp", axis=0, tiled=True),
    )
    blocks = tokens.reshape(rows_here, blocks_here, BLK)
    partners = [blocks]
    for level in range(LOG):
        if 1 << level < blocks_here:
            partners.append(flip_blocks(blocks, 1 << level))
        else:
            partners.append(swapped(blocks, "tensor", level - shift_bits))
    stacked = jnp.stack(partners)
    weight_blocks = weights.reshape(blocks_here, group_ratio, LOG + 1, BLK, BLK)
    preact = jnp.einsum(
        "ktqi,qrkio->tqro", stacked, weight_blocks, preferred_element_type=jnp.float32
    )
    preact = preact.reshape(rows_here, hidden_blocks * BLK)
    low_part = jnp.dot(tokens, left_full, preferred_element_type=jnp.float32)
    low_rank = lax.psum(low_part.astype(jnp.bfloat16), "tensor")
    preact = preact + jnp.dot(low_rank, right_full, preferred_element_type=jnp.float32)
    activation, slopes = gelu_pair(preact)
    hidden = activation.astype(jnp.bfloat16)
    grad_pre = (cotangent.astype(jnp.float32) * slopes).astype(jnp.bfloat16)
    grad_wide = grad_pre.reshape(rows_here, blocks_here, group_ratio, BLK)
    grad_weight = jnp.einsum(
        "ktqi,tqro->qrkio", stacked, grad_wide, preferred_element_type=jnp.float32
    )
    grad_weight = grad_weight.reshape(hidden_blocks, LOG + 1, BLK, BLK)
    low_back = jnp.einsum("th,rh->tr", grad_pre, right_full, preferred_element_type=jnp.float32)
    grad_low = lax.psum(low_back.astype(jnp.bfloat16), "tensor")
    grad_first = jnp.einsum("td,tr->dr", tokens, grad_low, preferred_element_type=jnp.float32)
    grad_second = jnp.einsum("tr,th->rh", low_rank, grad_pre, preferred_element_type=jnp.float32)
    returned = jnp.einsum(
        "tqro,qrkio->ktqi", grad_wide, weight_blocks, preferred_element_type=jnp.float32
    )
    summed = returned[0]
    for level in range(LOG):
        contrib = returned[level + 1]
        if 1 << level < blocks_here:
            summed = summed + flip_blocks(contrib, 1 << level)
        else:
            summed = summed + swapped(
                contrib.astype(jnp.bfloat16), "tensor", level - shift_bits
            ).astype(contrib.dtype)
    grad_input = summed.reshape(rows_here, blocks_here * BLK)
    grad_input = grad_input + jnp.einsum(
        "tr,dr->td", grad_low, left_full, preferred_element_type=jnp.float32
    )
    sum_weight, sum_first, sum_second = (
        lax.psum_scatter(
            grad_weight.astype(jnp.bfloat16), "dp", scatter_dimension=2, tiled=True
        ).astype(jnp.float32),
        lax.psum_scatter(
            grad_first.astype(jnp.bfloat16), "dp", scatter_dimension=0, tiled=True
        ).astype(jnp.float32),
        lax.psum_scatter(
            grad_second.astype(jnp.bfloat16), "dp", scatter_dimension=0, tiled=True
        ).astype(jnp.float32),
    )
    return (
        hidden,
        grad_input.astype(jnp.bfloat16),
        sum_weight.astype(jnp.bfloat16),
        sum_first.astype(jnp.bfloat16),
        sum_second.astype(jnp.bfloat16),
    )


def solution(mesh):
    placed = (
        P("dp", "tensor"),
        P("tensor", None, "dp", None),
        P(("tensor", "dp"), None),
        P("dp", "tensor"),
        P("dp", "tensor"),
    )
    return jax.shard_map(
        per_device,
        mesh=mesh,
        in_specs=placed,
        out_specs=(
            P("dp", "tensor"),
            P("dp", "tensor"),
            P("tensor", None, "dp", None),
            P(("tensor", "dp"), None),
            P("dp", "tensor"),
        ),
        check_vma=False,
    )
```

profile of v0, /device:TPU:0, one launch (start us, length us, event | category | flops | bytes accessed | tf_op | source)
XLA Modules:
  0.0 386.7 jit_solution(5141714083734337590)
XLA Ops:
  8.8 16.8 %all_gather.10 = bf16[1024,256]{1,0:T(8,128)(2,1)S(1)} all-gather(bf16[128,256]{1,0:T(8,128)(2,1)} %param.7), channel_id=1, replica_groups=mesh['dp'=8,'tensor'=4] {'dp'}, dimensions={0}, use_global_device_ids=true | all-gather | bytes 589824 | tf_op jit(solution)/shard_map/all_gather | solution.py:45
  26.4 2.4 convolution_convert_fusion.4
  39.1 2.3 copy.42
  42.8 2.4 copy.41
  45.2 2.3 rev.16
  48.5 2.3 constant_dynamic-update-slice_fusion.1
  51.8 8.5 %collective-permute-done = bf16[512,4,256]{2,0,1:T(8,128)(2,1)} collective-permute-done((bf16[512,4,256]{2,0,1:T(8,128)(2,1)}, bf16[512,4,256]{2,0,1:T(8,128)(2,1)}, u32[]{:S(2)}, u32[]{:S(2)}) %collective-permute-start) | collective-permute-done | bytes 1048608 | tf_op jit(solution)/shard_map/ppermute | solution.py:21
  60.3 2.3 bitcast_dynamic-update-slice_fusion.1
  62.6 2.3 bitcast_dynamic-update-slice_fusion
  64.8 47.8 %all-gather.3.cloned.1.call-done = bf16[16,5,256,256]{3,2,1,0:T(8,128)(2,1)} async-done(((bf16[16,5,32,256]{3,2,1,0:T(8,128)(2,1)}), bf16[16,5,256,256]{3,2,1,0:T(8,128)(2,1)}) %all-gather.3.cloned.1.call-update) | async-done | bytes 10485776 | tf_op jit(solution)/shard_map/all_gather | solution.py:44
  112.6 11.9 %fusion.6 = f32[4,512,4,256,1]{1,3,4,2,0:T(8,128)} fusion(bf16[4,4,5,256,256]{4,3,2,1,0:T(8,128)(2,1)} %bitcast.93, bf16[5,512,4,256]{3,1,0,2:T(8,128)(2,1)} %bitcast_dynamic-update-slice_fusion), kind=kOutput, calls=%fused_computation.11 | convolution fusion | flops 5368709120 | bytes 24117248 | tf_op jit(solution)/shard_map/ktqi,qrkio->tqro/dot_general | solution.py:57
  124.5 9.0 %copy.48 = f32[512,4096]{1,0:T(8,128)} copy(f32[512,4096]{0,1:T(8,128)} %bitcast.88) | data formatting | bytes 16777216 | tf_op jit(solution)/shard_map/reshape | solution.py:60
  133.5 8.6 %all-gather.5.cloned.1.call-done = bf16[256,4096]{1,0:T(8,128)(2,1)} async-done(((bf16[32,4096]{1,0:T(8,128)(2,1)}), bf16[256,4096]{1,0:T(8,128)(2,1)}) %all-gather.5.cloned.1.call-update) | async-done | bytes 2097168 | tf_op jit(solution)/shard_map/all_gather | solution.py:46
  142.1 10.0 %fusion.4 = (bf16[512,4096]{1,0:T(8,128)(2,1)S(1)}, bf16[512,4096]{1,0:T(8,128)(2,1)}) fusion(bf16[512,4096]{1,0:T(8,128)(2,1)} %param.9, f32[512,4096]{1,0:T(8,128)} %copy.48, bf16[512,256]{1,0:T(8,128)(2,1)} %all-reduce.3.cloned.1.call-done, bf16[256,4096]{1,0:T(8,128)(2,1)} %all-gather.5.cloned.1.call-done), kind=kOutput, calls=%fused_computation.5 | convolution fusion | flops 1103101952 | bytes 23330816 | tf_op jit(solution)/shard_map/dot_general | solution.py:63
  152.1 2.1 copy-done.1
  154.2 2.0 convolution_convert_fusion.3
  156.3 42.0 %all-reduce.5.cloned.1.call-done = bf16[512,256]{1,0:T(8,128)(2,1)} async-done(((bf16[512,256]{1,0:T(8,128)(2,1)}), bf16[512,256]{1,0:T(8,128)(2,1)}) %all-reduce.5.cloned.1.call-update) | async-done | bytes 262160 | tf_op jit(solution)/shard_map/psum | solution.py:73
  200.9 4.8 %convolution_convert_fusion.1 = bf16[256,4096]{1,0:T(8,128)(2,1)} fusion(bf16[512,256]{1,0:T(8,128)(2,1)S(1)} %copy-done.6, bf16[512,4096]{1,0:T(8,128)(2,1)} %copy-done.1), kind=kOutput, calls=%fused_computation.13 | convolution fusion | flops 1074790400 | bytes 6553600 | tf_op jit(solution)/shard_map/tr,th->rh/dot_general | solution.py:75
  205.8 7.9 %reshape.38 = bf16[512,4,4,256]{3,2,1,0:T(4,128)(2,1)} reshape(bf16[512,4096]{1,0:T(8,128)(2,1)} %copy-done.1) | data formatting | bytes 8388608 | tf_op jit(solution)/shard_map/reshape | solution.py:67
  213.7 7.5 %copy.62 = bf16[512,4,4,256,1]{0,3,4,2,1:T(8,128)(2,1)} copy(bf16[512,4,4,256,1]{3,2,1,0,4:T(4,128)(2,1)} %bitcast.83) | data formatting | bytes 8388608 | tf_op jit(solution)/shard_map/reshape | solution.py:67
  221.2 11.3 %convolution_convert_fusion = bf16[4,4,256,5,256]{4,2,3,1,0:T(8,128)(2,1)} fusion(bf16[512,4,4,256,1]{0,3,4,2,1:T(8,128)(2,1)} %copy.62, bf16[5,512,4,256]{3,1,0,2:T(8,128)(2,1)} %bitcast_dynamic-update-slice_fusion), kind=kOutput, calls=%fused_computation.9 | convolution fusion | flops 5373952000 | bytes 19922944 | tf_op jit(solution)/shard_map/ktqi,tqro->qrkio/dot_general | solution.py:68
  232.4 15.2 %copy.55 = bf16[16,5,256,256]{3,2,1,0:T(8,128)(2,1)} copy(bf16[16,5,256,256]{2,3,1,0:T(8,128)(2,1)} %bitcast.84) | data formatting | bytes 20971520 | tf_op jit(solution)/shard_map/convert_element_type | solution.py:94
  247.6 12.8 %fusion.14 = (bf16[5,512,4,256]{1,3,0,2:T(8,128)(2,1)}, f32[5,512,4,256]{1,3,0,2:T(8,128)}) fusion(bf16[512,4,4,256,1]{0,3,4,2,1:T(8,128)(2,1)} %copy.62, bf16[4,4,5,256,256]{4,3,2,1,0:T(8,128)(2,1)} %bitcast.94), kind=kOutput, calls=%fused_computation.33 | convolution fusion | flops 5371330560 | bytes 30408704 | tf_op jit(solution)/shard_map/tqro,qrkio->ktqi/dot_general | solution.py:76
  260.4 3.1 slice_bitcast_fusion.2
  265.6 4.7 %fusion.13 = (f32[1,512,4,256]{1,3,0,2:T(8,128)}, f32[1,512,4,256]{1,3,0,2:T(8,128)}) fusion(f32[5,512,4,256]{1,3,0,2:T(8,128)} %get-tuple-element.27), kind=kLoop, calls=%fused_computation.32 | loop fusion | bytes 8388608 | tf_op jit(solution)/shard_map/slice | solution.py:81
  270.2 1.8 rev.18
  272.0 3.1 rev.19
  276.9 11.3 %collective-permute-done.2 = bf16[512,4,256]{0,2,1:T(8,128)(2,1)} collective-permute-done((bf16[512,4,256]{0,2,1:T(8,128)(2,1)}, bf16[512,4,256]{0,2,1:T(8,128)(2,1)}, u32[]{:S(2)}, u32[]{:S(2)}) %collective-permute-start.2) | collective-permute-done | bytes 1048608 | tf_op jit(solution)/shard_map/ppermute | solution.py:21
  289.6 5.0 %fusion.11 = f32[512,4,256]{0,2,1:T(8,128)} fusion(f32[5,512,4,256]{1,3,0,2:T(8,128)} %get-tuple-element.27, f32[512,1,2,2,256]{0,4,3,2,1:T(8,128)} %rev.19, f32[512,2,2,1,256]{0,4,2,1,3:T(8,128)S(1)} %rev.18, bf16[512,4,256]{0,2,1:T(8,128)(2,1)} %collective-permute-done.3, bf16[512,4,256]{0,2,1:T(8,128)(2,1)} %collective-permute-done.2), kind=kLoop, calls=%fused_computation.19 | loop fusion | flops 3145728 | bytes 10485760 | tf_op jit(solution)/shard_map/add | solution.py:85
  294.6 3.1 copy.53
  297.7 2.9 add_convert_fusion
  300.6 79.1 %reduce-scatter.6.cloned.1.call-done = bf16[16,5,32,256]{3,2,1,0:T(8,128)(2,1)} async-done(((bf16[16,5,256,256]{3,2,1,0:T(8,128)(2,1)}), bf16[16,5,32,256]{3,2,1,0:T(8,128)(2,1)}) %reduce-scatter.6.cloned.1.call-update) | async-done | bytes 1310736 | tf_op jit(solution)/shard_map/reduce_scatter | solution.py:93
  (49 shorter events, 23.3 us)
Async XLA Ops:
  8.0 27.5 %copy-start = (bf16[512,1024]{1,0:T(8,128)(2,1)S(1)}, bf16[512,1024]{1,0:T(8,128)(2,1)}, u32[]{:S(2)}) copy-start(bf16[512,1024]{1,0:T(8,128)(2,1)} %param.5) | copy-start | bytes 3145732
  8.0 104.6 %all-gather.3.cloned.1.call-start = ((), (), s32[]{:S(2)}) async-start(), calls=%async_computation.3 | async-start | bytes 11796480 | tf_op jit(solution)/shard_map/all_gather | solution.py:44
  8.7 124.8 %all-reduce.3.cloned.1.call-start = ((), (), s32[]{:S(2)}) async-start(), calls=%async_computation.4 | async-start | bytes 524288 | tf_op jit(solution)/shard_map/psum | solution.py:62
  25.6 0.8 copy-start.3
  28.8 113.3 %all-gather.5.cloned.1.call-start = ((), (), s32[]{:S(2)}) async-start(), calls=%async_computation.5 | async-start | bytes 2359296 | tf_op jit(solution)/shard_map/all_gather | solution.py:46
  29.6 168.7 %all-reduce.5.cloned.1.call-start = ((), (), s32[]{:S(2)}) async-start(), calls=%async_computation.6 | async-start | bytes 524288 | tf_op jit(solution)/shard_map/psum | solution.py:73
  32.5 27.8 %collective-permute-start = (bf16[512,4,256]{2,0,1:T(8,128)(2,1)}, bf16[512,4,256]{2,0,1:T(8,128)(2,1)}, u32[]{:S(2)}, u32[]{:S(2)}) collective-permute-start(bf16[512,4,256]{2,0,1:T(8,128)(2,1)} %copy.44), channel_id=1, source_target_pairs={{0,1},{1,0},{2,3},{3,2},{4,5},{5,4},{6,7},{7,6},{8,9},{9,8},{10,11... | collective-permute-start | bytes 3145736 | tf_op jit(solution)/shard_map/ppermute | solution.py:21
  34.0 28.6 %collective-permute-start.1 = (bf16[512,4,256]{2,0,1:T(8,128)(2,1)}, bf16[512,4,256]{2,0,1:T(8,128)(2,1)}, u32[]{:S(2)}, u32[]{:S(2)}) collective-permute-start(bf16[512,4,256]{2,0,1:T(8,128)(2,1)} %copy.44), channel_id=1, source_target_pairs={{0,2},{2,0},{1,3},{3,1},{4,6},{6,4},{5,7},{7,5},{8,10},{10,8},{9,1... | collective-permute-start | bytes 3145736 | tf_op jit(solution)/shard_map/ppermute | solution.py:21
  142.1 12.1 %copy-start.7 = (bf16[256,4096]{1,0:T(8,128)(2,1)S(1)}, bf16[256,4096]{1,0:T(8,128)(2,1)}, u32[]{:S(2)}) copy-start(bf16[256,4096]{1,0:T(8,128)(2,1)} %all-gather.5.cloned.1.call-done) | copy-start | bytes 6291460
  152.1 2.1 copy-start.1
  154.2 46.7 %copy-start.6 = (bf16[512,256]{1,0:T(8,128)(2,1)S(1)}, bf16[512,256]{1,0:T(8,128)(2,1)}, u32[]{:S(2)}) copy-start(bf16[512,256]{1,0:T(8,128)(2,1)} %all-reduce.3.cloned.1.call-done) | copy-start | bytes 786436
  156.2 144.3 %reduce-scatter.10.cloned.1.call-start = ((), (), s32[]{:S(2)}) async-start(), calls=%async_computation.9 | async-start | bytes 589824
  200.7 99.9 %reduce-scatter.8.cloned.1.call-start = ((), (), s32[]{:S(2)}) async-start(), calls=%async_computation.8 | async-start | bytes 2359296 | tf_op jit(solution)/shard_map/reduce_scatter | solution.py:99
  205.8 173.8 %reduce-scatter.6.cloned.1.call-start = ((), (), s32[]{:S(2)}) async-start(), calls=%async_computation.7 | async-start | bytes 11796480 | tf_op jit(solution)/shard_map/reduce_scatter | solution.py:93
  263.5 24.7 %collective-permute-start.2 = (bf16[512,4,256]{0,2,1:T(8,128)(2,1)}, bf16[512,4,256]{0,2,1:T(8,128)(2,1)}, u32[]{:S(2)}, u32[]{:S(2)}) collective-permute-start(bf16[512,4,256]{0,2,1:T(8,128)(2,1)} %get-tuple-element.24), channel_id=1, source_target_pairs={{0,1},{1,0},{2,3},{3,2},{4,5},{5,4},{6,7},{7,6},{8,9},{9,8},{10,11... | collective-permute-start | bytes 3145736 | tf_op jit(solution)/shard_map/ppermute | solution.py:21
  265.0 24.6 %collective-permute-start.3 = (bf16[512,4,256]{0,2,1:T(8,128)(2,1)}, bf16[512,4,256]{0,2,1:T(8,128)(2,1)}, u32[]{:S(2)}, u32[]{:S(2)}) collective-permute-start(bf16[512,4,256]{0,2,1:T(8,128)(2,1)} %get-tuple-element.25), channel_id=1, source_target_pairs={{0,2},{2,0},{1,3},{3,1},{4,6},{6,4},{5,7},{7,5},{8,10},{10,8},{9,1... | collective-permute-start | bytes 3145736 | tf_op jit(solution)/shard_map/ppermute | solution.py:21
  270.2 4.9 %copy-start.4 = (bf16[1024,256]{1,0:T(8,128)(2,1)S(1)}, bf16[1024,256]{1,0:T(8,128)(2,1)}, u32[]{:S(2)}) copy-start(bf16[1024,256]{1,0:T(8,128)(2,1)} %copy-done.3) | copy-start | bytes 1572868
  270.2 4.9 %copy-start.5 = (bf16[512,256]{1,0:T(8,128)(2,1)S(1)}, bf16[512,256]{1,0:T(8,128)(2,1)}, u32[]{:S(2)}) copy-start(bf16[512,256]{1,0:T(8,128)(2,1)} %all-reduce.5.cloned.1.call-done) | copy-start | bytes 786436
  294.6 3.1 copy-start.2
Sparse Core Ops, SparseCore 0:
  10.4 102.0 all-gather.2
  114.3 27.8 all-gather.4
  200.8 30.9 reduce-scatter.9
  234.6 33.9 reduce-scatter.7
  271.5 108.0 reduce-scatter.5
Sparse Core Ops, SparseCore 1:
  28.9 46.1 all-reduce.2
  156.3 41.9 all-reduce.4
where the time goes:
time: 388 us; the launch traced here: 387 us
  waiting for transfers between devices  200 us (52%)
  local copies, waits for them, and re-layouts  82.8 us (21%)
  matrix products  58.3 us (15%)
  blocking collectives  16.8 us (4%)
  between operations  15.3 us (4%)
  other arithmetic  7.92 us (2%)
  starting transfers between devices  5.51 us (1%)
    reduce_scatter x1, waiting for transfers between devices, per_device(): lax.psum_scatter(grad_weight.astype(jnp.bfloat16), 'dp', scatter_dimensio...  79.1 us
    all_gather x1, waiting for transfers between devices, per_device(): lax.all_gather(butterfly, 'dp', axis=2, tiled=True)  47.8 us
    psum x1, waiting for transfers between devices, per_device(): grad_low = lax.psum(low_back.astype(jnp.bfloat16), 'tensor')  42 us
    ppermute x4, waiting for transfers between devices, swapped(): return lax.ppermute(block, axis, route)  21.2 us
    all_gather x1, blocking collectives, per_device(): lax.all_gather(left_factor, 'dp', axis=0, tiled=True)  16.8 us
    reshape x2, local copies, waits for them, and re-layouts, per_device(): grad_wide = grad_pre.reshape(rows_here, blocks_here, group_ratio, BLK)  15.4 us
    convert_element_type x1, local copies, waits for them, and re-layouts, per_device(): grad_weight.astype(jnp.bfloat16)  15.2 us
    dot_general x1, matrix products, per_device(): jnp.einsum('tqro,qrkio->ktqi', grad_wide, weight_blocks, preferred_elemen...  12.8 us
  transfers between devices with their start and end apart: 11, of which 7 were waited for; matrix products, arithmetic and copies ran while one was open for 34% of the time, Pallas kernels for 0%

commit v1 on v0

v1 whole, which is shorter than its diff:
```python
import functools

import jax
import jax.numpy as jnp
from jax import lax
from jax.experimental import pallas as pl
from jax.experimental.pallas import tpu as pltpu
from jax.sharding import PartitionSpec as P

BLK = 256
LOG = 4


ROOT_HALF = 0.7071067811865476
INV_ROOT_TWO_PI = 0.3989422804014327
BF16 = jnp.bfloat16
F32 = jnp.float32


def swapped(block, axis, mask):
    count = lax.axis_size(axis)
    return lax.ppermute(block, axis, [(i, i ^ mask) for i in range(count)])


def summed_over(part, axis):
    count = lax.axis_size(axis)
    total = part.astype(F32)
    for mask in range(1, count):
        total = total + swapped(part, axis, mask).astype(F32)
    return total.astype(BF16)


def gelu_pair(preact):
    cdf = 0.5 * (1.0 + lax.erf(preact * ROOT_HALF))
    return (preact * cdf, cdf + preact * INV_ROOT_TWO_PI * jnp.exp(-0.5 * preact * preact))


def nt_dot(a, b):
    return lax.dot_general(a, b, (((1,), (1,)), ((), ())), preferred_element_type=F32)


def chunk_kernel(factors, local, aliased, *refs):
    pieces = refs[:factors]
    cot_ref, w_ref = refs[factors:factors + 2]
    rest = refs[factors + 2 + (1 if aliased else 0):]
    hidden_ref, dw_ref, loc_ref = rest[:3]
    far_refs = rest[3:3 + factors - 1 - local]
    low_ref = rest[3 + factors - 1 - local]
    x, xt, acc = rest[-3:]
    step = pl.program_id(0)

    @pl.when(step == 0)
    def _():
        for k in range(factors):
            piece = pieces[k][...]
            x[:, k * BLK:(k + 1) * BLK] = piece
            xt[k * BLK:(k + 1) * BLK, :] = piece.T

    w = w_ref[0]
    preact = jnp.dot(x[...], w, preferred_element_type=F32)
    act, slope = gelu_pair(preact)
    hidden_ref[...] = act.astype(BF16)
    grad = (cot_ref[...].astype(F32) * slope).astype(BF16)
    dw_ref[0] = jnp.dot(xt[...], grad, preferred_element_type=F32).astype(BF16)
    back = nt_dot(grad, w)

    @pl.when(step == 0)
    def _():
        acc[...] = back

    @pl.when(step > 0)
    def _():
        acc[...] += back

    @pl.when(step == pl.num_programs(0) - 1)
    def _():
        loc_ref[...] = acc[:, :local * BLK]
        for i, far in enumerate(far_refs):
            far[...] = acc[:, (local + i) * BLK:(local + i + 1) * BLK].astype(BF16)
        low_ref[...] = acc[:, (factors - 1) * BLK:]


def run_chunk(q, ratio, local, piece_arrays, piece_cols, cot, w, hidden_prev):
    rows, wide = cot.shape
    factors = len(piece_arrays)
    depth = factors * BLK
    n_far = factors - 1 - local
    column = lambda col: pl.BlockSpec((rows, BLK), lambda h: (0, col))
    in_specs = [column(col) for col in piece_cols]
    in_specs += [
        pl.BlockSpec((rows, BLK), lambda h: (0, q * ratio + h)),
        pl.BlockSpec((1, depth, BLK), lambda h: (h, 0, 0)),
    ]
    args = list(piece_arrays) + [cot, w]
    aliases = {}
    if hidden_prev is not None:
        aliases = {len(args): 0}
        args.append(hidden_prev)
        in_specs.append(pl.BlockSpec(memory_space=pl.ANY))
    whole = lambda cols: pl.BlockSpec((rows, cols), lambda h: (0, 0))
    out_specs = [
        pl.BlockSpec((rows, BLK), lambda h: (0, q * ratio + h)),
        pl.BlockSpec((1, depth, BLK), lambda h: (h, 0, 0)),
        whole(local * BLK),
    ] + [whole(BLK)] * (n_far + 1)
    out_shape = [
        jax.ShapeDtypeStruct((rows, wide), BF16),
        jax.ShapeDtypeStruct((ratio, depth, BLK), BF16),
        jax.ShapeDtypeStruct((rows, local * BLK), F32),
    ] + [jax.ShapeDtypeStruct((rows, BLK), BF16)] * n_far + [jax.ShapeDtypeStruct((rows, BLK), F32)]
    return pl.pallas_call(
        functools.partial(chunk_kernel, factors, local, hidden_prev is not None),
        grid=(ratio,),
        in_specs=in_specs,
        out_specs=out_specs,
        out_shape=out_shape,
        scratch_shapes=[
            pltpu.VMEM((rows, depth), BF16),
            pltpu.VMEM((depth, rows), BF16),
            pltpu.VMEM((rows, depth), F32),
        ],
        input_output_aliases=aliases,
        cost_estimate=pl.CostEstimate(
            flops=6 * rows * depth * BLK * ratio,
            bytes_accessed=2 * (2 * ratio * depth * BLK + 2 * rows * ratio * BLK + 5 * rows * depth // 2),
            transcendentals=2 * rows * ratio * BLK,
        ),
        compiler_params=pltpu.CompilerParams(
            dimension_semantics=("arbitrary",), vmem_limit_bytes=40 * 1024 * 1024
        ),
    )(*args)


def final_kernel(blocks, local_masks, n_far, *refs):
    locs = refs[:blocks]
    fars = refs[blocks:blocks + n_far * blocks]
    grad_low, left, out = refs[blocks + n_far * blocks:]
    for j in range(blocks):
        total = nt_dot(grad_low[...], left[j * BLK:(j + 1) * BLK, :])
        for k, mask in enumerate(local_masks):
            total = total + locs[j ^ mask][:, k * BLK:(k + 1) * BLK]
        for i in range(n_far):
            total = total + fars[i * blocks + j][...].astype(F32)
        out[:, j * BLK:(j + 1) * BLK] = total.astype(BF16)


def per_device(tokens, butterfly, left_factor, right_factor, cotangent):
    rows = tokens.shape[0]
    blocks = tokens.shape[1] // BLK
    hidden_blocks = right_factor.shape[1] // BLK
    share = right_factor.shape[0]
    ratio = hidden_blocks // blocks
    local_masks = [0] + [1 << b for b in range(LOG) if 1 << b < blocks]
    far_masks = [(1 << b) // blocks for b in range(LOG) if 1 << b >= blocks]
    n_far = len(far_masks)
    factors = LOG + 2

    right_blocks = right_factor.reshape(share, hidden_blocks, BLK).transpose(1, 0, 2)
    weights = []
    for q in range(blocks):
        part = slice(q * ratio, (q + 1) * ratio)
        local_w = jnp.concatenate([butterfly[part], right_blocks[part][:, None]], axis=1)
        full = lax.all_gather(local_w, "dp", axis=2, tiled=True)
        weights.append(full.reshape(ratio, factors * BLK, BLK))

    left_full = lax.all_gather(left_factor, "dp", axis=0, tiled=True)
    far_tokens = [swapped(tokens, "tensor", mask) for mask in far_masks]
    low_part = jnp.dot(tokens, left_full, preferred_element_type=F32).astype(BF16)
    low = summed_over(low_part, "tensor")

    hidden = None
    locs, fars, low_back, grads = [], [[] for _ in far_masks], None, []
    for q in range(blocks):
        arrays = [tokens] * len(local_masks) + far_tokens + [low]
        columns = [q ^ mask for mask in local_masks] + [q] * n_far + [0]
        hidden, dw, loc, *more = run_chunk(
            q, ratio, len(local_masks), arrays, columns, cotangent, weights[q], hidden
        )
        grads.append(
            lax.psum_scatter(
                dw.reshape(ratio, factors, BLK, BLK), "dp", scatter_dimension=2, tiled=True
            )
        )
        locs.append(loc)
        for i, mask in enumerate(far_masks):
            fars[i].append(swapped(more[i], "tensor", mask))
        low_back = more[-1] if low_back is None else low_back + more[-1]

    grad_low = summed_over(low_back.astype(BF16), "tensor")
    grad_first = jnp.einsum("td,tr->dr", tokens, grad_low, preferred_element_type=F32)
    sum_first = lax.psum_scatter(grad_first.astype(BF16), "dp", scatter_dimension=0, tiled=True)
    grad_tokens = pl.pallas_call(
        functools.partial(final_kernel, blocks, local_masks, n_far),
        out_shape=jax.ShapeDtypeStruct(tokens.shape, BF16),
        in_specs=[pl.BlockSpec(memory_space=pltpu.VMEM)] * (blocks + n_far * blocks + 2),
        out_specs=pl.BlockSpec(memory_space=pltpu.VMEM),
        cost_estimate=pl.CostEstimate(
            flops=2 * rows * blocks * BLK * BLK,
            bytes_accessed=rows * blocks * BLK * (4 * len(local_masks) + 2 * n_far + 2),
            transcendentals=0,
        ),
        compiler_params=pltpu.CompilerParams(vmem_limit_bytes=40 * 1024 * 1024),
    )(*locs, *[f for level in fars for f in level], grad_low, left_full)

    grad_all = jnp.concatenate(grads, axis=0)
    sum_weight = grad_all[:, :LOG + 1]
    sum_second = grad_all[:, LOG + 1].transpose(1, 0, 2).reshape(share, hidden_blocks * BLK)
    return (hidden, grad_tokens, sum_weight, sum_first, sum_second)


def solution(mesh):
    placed = (
        P("dp", "tensor"),
        P("tensor", None, "dp", None),
        P(("tensor", "dp"), None),
        P("dp", "tensor"),
        P("dp", "tensor"),
    )
    return jax.shard_map(
        per_device,
        mesh=mesh,
        in_specs=placed,
        out_specs=(
            P("dp", "tensor"),
            P("dp", "tensor"),
            P("tensor", None, "dp", None),
            P(("tensor", "dp"), None),
            P("dp", "tensor"),
        ),
        check_vma=False,
    )
```

time: 388 us -> 377 us (0.972)
  matrix products: 58.3 us -> 1.7 us
  Pallas kernels: 0 us -> 55.8 us
  local copies, waits for them, and re-layouts: 82.8 us -> 40.6 us
  waiting for transfers between devices: 200 us -> 219 us
  starting transfers between devices: 5.51 us -> 22.2 us
    dot_general x9 -> x2, matrix products: 58.3 us -> 1.7 us  [the longest x1 1.27 us: per_device(): jnp.einsum('td,tr->dr', tokens, grad_low, preferred_element_type=F32)]
    pallas_call x0 -> x5, Pallas kernels: none -> 55.8 us  [the longest x4 53 us: run_chunk(): pl.pallas_call(functools.partial(chunk_kernel, factors, local, hidden_pre...]
    psum x2 -> x0, waiting for transfers between devices: 42 us -> none  [the longest x1 42 us: per_device(): grad_low = lax.psum(low_back.astype(jnp.bfloat16), 'tensor')]
    unnamed x8 -> x10, waiting for transfers between devices: 1.46 us -> 30.1 us
    reshape x5 -> x2, local copies, waits for them, and re-layouts: 28.8 us -> 0.74 us  [the longest x1 0.72 us: per_device(): grad_all[:, LOG + 1].transpose(1, 0, 2).reshape(share, hidden_blocks * BLK)]
    unnamed x22 -> x63, local copies, waits for them, and re-layouts: 12 us -> 36.2 us
    convert_element_type x2 -> x0, local copies, waits for them, and re-layouts: 18.2 us -> none  [the longest x1 15.2 us: per_device(): grad_weight.astype(jnp.bfloat16)]
    reduce_scatter x2 -> x4, waiting for transfers between devices: 79.1 us -> 97.1 us  [per_device(): lax.psum_scatter(dw.reshape(ratio, factors, BLK, BLK), 'dp', scatter_dime...]
  transfers between devices with their start and end apart: 11 -> 25, of which waited for: 7 -> 18; matrix products, arithmetic and copies ran while one was open for 34% -> 4% of each run, Pallas kernels for 0% -> 15%
where the time goes in v1:
time: 377 us; the launch traced here: 376 us
  waiting for transfers between devices  219 us (58%)
  Pallas kernels  55.8 us (15%)
  local copies, waits for them, and re-layouts  40.6 us (11%)
  starting transfers between devices  22.2 us (6%)
  blocking collectives  17.1 us (5%)
  between operations  14 us (4%)
  other arithmetic  5.08 us (1%)
    reduce_scatter x4, waiting for transfers between devices, per_device(): lax.psum_scatter(dw.reshape(ratio, factors, BLK, BLK), 'dp', scatter_dime...  97.1 us
    all_gather x4, waiting for transfers between devices, per_device(): full = lax.all_gather(local_w, 'dp', axis=2, tiled=True)  57.9 us
    pallas_call x4, Pallas kernels, run_chunk(): pl.pallas_call(functools.partial(chunk_kernel, factors, local, hidden_pre...  53 us
    unnamed x63, local copies, waits for them, and re-layouts  36.2 us
    ppermute x16, waiting for transfers between devices, swapped(): return lax.ppermute(block, axis, [(i, i ^ mask) for i in range(count)])  34 us
    unnamed x10, waiting for transfers between devices  30.1 us
    ppermute x16, starting transfers between devices, swapped(): return lax.ppermute(block, axis, [(i, i ^ mask) for i in range(count)])  21.6 us
    all_gather x1, blocking collectives, per_device(): left_full = lax.all_gather(left_factor, 'dp', axis=0, tiled=True)  17.1 us
  transfers between devices with their start and end apart: 25, of which 18 were waited for; matrix products, arithmetic and copies ran while one was open for 4% of the time, Pallas kernels for 15%

profile of v1, /device:TPU:0, one launch (start us, length us, event | category | flops | bytes accessed | tf_op | source)
XLA Modules:
  0.0 375.6 jit_solution(3277119784135712654)
XLA Ops:
  12.2 3.0 collective-permute-start
  15.2 1.5 collective-permute-start.1
  16.7 17.1 %all_gather.15.refs_13_ = bf16[1024,256]{1,0:T(8,128)(2,1)S(1)} all-gather(bf16[128,256]{1,0:T(8,128)(2,1)S(1)} %copy-done.28), channel_id=1, replica_groups=mesh['dp'=8,'tensor'=4] {'dp'}, dimensions={0}, use_global_device_ids=true | all-gather | bytes 589824 | tf_op jit(solution)/shard_map/all_gather | solution.py:166
  34.8 3.0 collective-permute-start.4
  37.8 7.0 %collective-permute-done.2 = bf16[512,256]{1,0:T(8,128)(2,1)S(1)} collective-permute-done((bf16[512,256]{1,0:T(8,128)(2,1)S(1)}, bf16[512,256]{1,0:T(8,128)(2,1)S(1)}, u32[]{:S(2)}, u32[]{:S(2)}) %collective-permute-start.2) | collective-permute-done | bytes 262176 | tf_op jit(solution)/shard_map/ppermute | solution.py:22
  44.8 6.2 %collective-permute-done.3 = bf16[512,256]{1,0:T(8,128)(2,1)S(1)} collective-permute-done((bf16[512,256]{1,0:T(8,128)(2,1)S(1)}, bf16[512,256]{1,0:T(8,128)(2,1)S(1)}, u32[]{:S(2)}, u32[]{:S(2)}) %collective-permute-start.3) | collective-permute-done | bytes 262176 | tf_op jit(solution)/shard_map/ppermute | solution.py:22
  53.8 1.9 copy-done.14
  58.1 13.2 %shard_map.92 = (bf16[512,4096]{1,0:T(8,128)(2,1)}, bf16[4,1536,256]{2,1,0:T(8,128)(2,1)}, f32[512,768]{1,0:T(8,128)S(1)}, bf16[512,256]{1,0:T(8,128)(2,1)}, bf1...) custom-call(bf16[512,1024]{1,0:T(8,128)(2,1)S(1)} %copy-done.6, bf16[512,1024]{1,0:T(8,128)(2,1)S(1)} %copy-done.6, ...), custom_call_target="tpu_custom_call" | custom-call | flops 4831838208 | bytes 12320768 | tf_op jit(solution)/shard_map/pallas_call | solution.py:111
  72.9 19.3 %all-gather.9.cloned.1.call-done = bf16[4,6,256,256]{3,2,1,0:T(8,128)(2,1)} async-done(((bf16[4,6,32,256]{3,2,1,0:T(8,128)(2,1)}), bf16[4,6,256,256]{3,2,1,0:T(8,128)(2,1)}) %all-gather.9.cloned.1.call-update) | async-done | bytes 3145744 | tf_op jit(solution)/shard_map/all_gather | solution.py:163
  92.2 1.9 copy-done.13
  96.5 13.3 %shard_map.93 = (bf16[512,4096]{1,0:T(8,128)(2,1)}, bf16[4,1536,256]{2,1,0:T(8,128)(2,1)}, f32[512,768]{1,0:T(8,128)S(1)}, bf16[512,256]{1,0:T(8,128)(2,1)}, bf1...) custom-call(bf16[512,1024]{1,0:T(8,128)(2,1)S(1)} %copy-done.6, ...), custom_call_target="tpu_custom_call", output_to_operand_aliasing={{0}: (8, {})} | custom-call | flops 4831838208 | bytes 12320768 | tf_op jit(solution)/shard_map/pallas_call | solution.py:111
  111.8 19.2 %all-gather.7.cloned.1.call-done = bf16[4,6,256,256]{3,2,1,0:T(8,128)(2,1)} async-done(((bf16[4,6,32,256]{3,2,1,0:T(8,128)(2,1)}), bf16[4,6,256,256]{3,2,1,0:T(8,128)(2,1)}) %all-gather.7.cloned.1.call-update) | async-done | bytes 3145744 | tf_op jit(solution)/shard_map/all_gather | solution.py:163
  131.0 1.9 copy-done.12
  135.3 13.3 %shard_map.94 = (bf16[512,4096]{1,0:T(8,128)(2,1)}, bf16[4,1536,256]{2,1,0:T(8,128)(2,1)}, f32[512,768]{1,0:T(8,128)S(1)}, bf16[512,256]{1,0:T(8,128)(2,1)}, bf1...) custom-call(bf16[512,1024]{1,0:T(8,128)(2,1)S(1)} %copy-done.6, ...), custom_call_target="tpu_custom_call", output_to_operand_aliasing={{0}: (8, {})} | custom-call | flops 4831838208 | bytes 12320768 | tf_op jit(solution)/shard_map/pallas_call | solution.py:111
  150.9 18.8 %all-gather.5.cloned.1.call-done = bf16[4,6,256,256]{3,2,1,0:T(8,128)(2,1)} async-done(((bf16[4,6,32,256]{3,2,1,0:T(8,128)(2,1)}), bf16[4,6,256,256]{3,2,1,0:T(8,128)(2,1)}) %all-gather.5.cloned.1.call-update) | async-done | bytes 3145744 | tf_op jit(solution)/shard_map/all_gather | solution.py:163
  169.6 1.9 copy-done.11
  174.0 13.3 %shard_map.95 = (bf16[512,4096]{1,0:T(8,128)(2,1)}, bf16[4,1536,256]{2,1,0:T(8,128)(2,1)}, f32[512,768]{1,0:T(8,128)S(1)}, bf16[512,256]{1,0:T(8,128)(2,1)}, bf1...) custom-call(bf16[512,1024]{1,0:T(8,128)(2,1)S(1)} %copy-done.6, ...), custom_call_target="tpu_custom_call", output_to_operand_aliasing={{0}: (8, {})} | custom-call | flops 4831838208 | bytes 12320768 | tf_op jit(solution)/shard_map/pallas_call | solution.py:111
  189.3 1.7 add_convert_fusion.1
  190.9 1.5 collective-permute-start.13
  194.5 1.5 collective-permute-start.12
  197.4 2.7 collective-permute-done.13
  201.6 5.7 %collective-permute-done.14 = bf16[512,256]{1,0:T(8,128)(2,1)S(1)} collective-permute-done((bf16[512,256]{1,0:T(8,128)(2,1)S(1)}, bf16[512,256]{1,0:T(8,128)(2,1)S(1)}, u32[]{:S(2)}, u32[]{:S(2)}) %collective-permute-start.14) | collective-permute-done | bytes 262176 | tf_op jit(solution)/shard_map/ppermute | solution.py:22
  208.7 2.1 copy.25
  215.0 3.6 collective-permute-done.11.refs_10_
  220.4 3.8 %collective-permute-done.10.refs_9_ = bf16[512,256]{1,0:T(8,128)(2,1)S(1)} collective-permute-done((bf16[512,256]{1,0:T(8,128)(2,1)}, bf16[512,256]{1,0:T(8,128)(2,1)S(1)}, u32[]{:S(2)}, u32[]{:S(2)}) %collective-permute-start.10) | collective-permute-done | bytes 262176 | tf_op jit(solution)/shard_map/ppermute | solution.py:22
  224.1 1.9 collective-permute-done.6.refs_5_
  226.0 2.8 collective-permute-done.5.refs_4_
  233.1 2.8 shard_map.96
  236.9 15.7 %reduce-scatter.10.cloned.1.call-done = bf16[4,6,32,256]{3,2,1,0:T(8,128)(2,1)} async-done(((bf16[4,6,256,256]{3,2,1,0:T(8,128)(2,1)}), bf16[4,6,32,256]{3,2,1,0:T(8,128)(2,1)}) %reduce-scatter.10.cloned.1.call-update) | async-done | bytes 393232 | tf_op jit(solution)/shard_map/reduce_scatter | solution.py:180
  253.6 40.7 %reduce-scatter.12.cloned.1.call-done = bf16[4,6,32,256]{3,2,1,0:T(8,128)(2,1)} async-done(((bf16[4,6,256,256]{3,2,1,0:T(8,128)(2,1)}), bf16[4,6,32,256]{3,2,1,0:T(8,128)(2,1)}) %reduce-scatter.12.cloned.1.call-update) | async-done | bytes 393232 | tf_op jit(solution)/shard_map/reduce_scatter | solution.py:180
  295.4 40.7 %reduce-scatter.14.cloned.1.call-done = bf16[4,6,32,256]{3,2,1,0:T(8,128)(2,1)} async-done(((bf16[4,6,256,256]{3,2,1,0:T(8,128)(2,1)}), bf16[4,6,32,256]{3,2,1,0:T(8,128)(2,1)}) %reduce-scatter.14.cloned.1.call-update) | async-done | bytes 393232 | tf_op jit(solution)/shard_map/reduce_scatter | solution.py:180
  339.1 30.0 %reduce-scatter.16.cloned.1.call-done = bf16[128,256]{1,0:T(8,128)(2,1)} async-done(((bf16[1024,256]{1,0:T(8,128)(2,1)}), bf16[128,256]{1,0:T(8,128)(2,1)}) %reduce-scatter.16.cloned.1.call-update) | async-done | bytes 65552
  (111 shorter events, 48.8 us)
Async XLA Ops:
  7.2 46.6 %all-gather.11.cloned.1.call-start = ((), (), s32[]{:S(2)}) async-start(), calls=%async_computation.8 | async-start | bytes 3538944 | tf_op jit(solution)/shard_map/all_gather | solution.py:163
  9.5 82.7 %all-gather.9.cloned.1.call-start = ((), (), s32[]{:S(2)}) async-start(), calls=%async_computation.7 | async-start | bytes 3538944 | tf_op jit(solution)/shard_map/all_gather | solution.py:163
  10.4 1.8 copy-start.6
  10.4 6.3 %copy-start.28 = (bf16[128,256]{1,0:T(8,128)(2,1)S(1)}, bf16[128,256]{1,0:T(8,128)(2,1)}, u32[]{:S(2)}) copy-start(bf16[128,256]{1,0:T(8,128)(2,1)} %param.7) | copy-start | bytes 196612
  10.4 120.6 %all-gather.7.cloned.1.call-start = ((), (), s32[]{:S(2)}) async-start(), calls=%async_computation.6 | async-start | bytes 3538944 | tf_op jit(solution)/shard_map/all_gather | solution.py:163
  11.3 158.4 %all-gather.5.cloned.1.call-start = ((), (), s32[]{:S(2)}) async-start(), calls=%async_computation.5 | async-start | bytes 3538944 | tf_op jit(solution)/shard_map/all_gather | solution.py:163
  12.1 223.8 %reduce-scatter.8.cloned.1.call-start = ((), (), s32[]{:S(2)}) async-start(), calls=%async_computation.9 | async-start | bytes 3538944 | tf_op jit(solution)/shard_map/reduce_scatter | solution.py:180
  12.2 39.0 %collective-permute-start = (bf16[512,1024]{1,0:T(8,128)(2,1)S(1)}, bf16[512,1024]{1,0:T(8,128)(2,1)S(1)}, u32[]{:S(2)}, u32[]{:S(2)}) collective-permute-start(bf16[512,1024]{1,0:T(8,128)(2,1)S(1)} %copy-done.6), channel_id=1, source_target_pairs={{0,1},{1,0},{2,3},{3,2},{4,5},{5,4},{6,7},{7,6},{8,9},{9,8},{10,11... | collective-permute-start | bytes 3145736 | tf_op jit(solution)/shard_map/ppermute | solution.py:22
  15.2 37.0 %collective-permute-start.1 = (bf16[512,1024]{1,0:T(8,128)(2,1)S(1)}, bf16[512,1024]{1,0:T(8,128)(2,1)S(1)}, u32[]{:S(2)}, u32[]{:S(2)}) collective-permute-start(bf16[512,1024]{1,0:T(8,128)(2,1)S(1)} %copy-done.6), channel_id=1, source_target_pairs={{0,2},{1,3},{2,0},{3,1},{4,6},{5,7},{6,4},{7,5},{8,10},{9,11},{10,... | collective-permute-start | bytes 3145736 | tf_op jit(solution)/shard_map/ppermute | solution.py:22
  34.2 10.6 %collective-permute-start.2 = (bf16[512,256]{1,0:T(8,128)(2,1)S(1)}, bf16[512,256]{1,0:T(8,128)(2,1)S(1)}, u32[]{:S(2)}, u32[]{:S(2)}) collective-permute-start(bf16[512,256]{1,0:T(8,128)(2,1)S(1)} %convolution_convert_fusion.1), channel_id=1, source_target_pairs={{0,1},{1,0},{2,3},{3,2},{4,5},{5,4},{6,7},{7,6},{8,9},{9,8},{10,11... | collective-permute-start | bytes 786440 | tf_op jit(solution)/shard_map/ppermute | solution.py:22
  34.6 16.4 %collective-permute-start.3 = (bf16[512,256]{1,0:T(8,128)(2,1)S(1)}, bf16[512,256]{1,0:T(8,128)(2,1)S(1)}, u32[]{:S(2)}, u32[]{:S(2)}) collective-permute-start(bf16[512,256]{1,0:T(8,128)(2,1)S(1)} %convolution_convert_fusion.1), channel_id=1, source_target_pairs={{0,2},{1,3},{2,0},{3,1},{4,6},{5,7},{6,4},{7,5},{8,10},{9,11},{10,... | collective-permute-start | bytes 786440 | tf_op jit(solution)/shard_map/ppermute | solution.py:22
  34.8 16.3 %collective-permute-start.4 = (bf16[512,256]{1,0:T(8,128)(2,1)S(1)}, bf16[512,256]{1,0:T(8,128)(2,1)S(1)}, u32[]{:S(2)}, u32[]{:S(2)}) collective-permute-start(bf16[512,256]{1,0:T(8,128)(2,1)S(1)} %convolution_convert_fusion.1), channel_id=1, source_target_pairs={{0,3},{1,2},{2,1},{3,0},{4,7},{5,6},{6,5},{7,4},{8,11},{9,10},{10,... | collective-permute-start | bytes 786440 | tf_op jit(solution)/shard_map/ppermute | solution.py:22
  53.8 1.9 copy-start.14
  72.8 179.8 %reduce-scatter.10.cloned.1.call-start = ((), (), s32[]{:S(2)}) async-start(), calls=%async_computation.10 | async-start | bytes 3538944 | tf_op jit(solution)/shard_map/reduce_scatter | solution.py:180
  92.2 1.9 copy-start.13
  111.8 182.6 %reduce-scatter.12.cloned.1.call-start = ((), (), s32[]{:S(2)}) async-start(), calls=%async_computation.11 | async-start | bytes 3538944 | tf_op jit(solution)/shard_map/reduce_scatter | solution.py:180
  131.0 1.9 copy-start.12
  150.6 185.5 %reduce-scatter.14.cloned.1.call-start = ((), (), s32[]{:S(2)}) async-start(), calls=%async_computation.12 | async-start | bytes 3538944 | tf_op jit(solution)/shard_map/reduce_scatter | solution.py:180
  169.6 1.9 copy-start.11
  189.2 179.8 %reduce-scatter.16.cloned.1.call-start = ((), (), s32[]{:S(2)}) async-start(), calls=%async_computation.13 | async-start | bytes 589824
  190.9 9.2 %collective-permute-start.13 = (bf16[512,256]{1,0:T(8,128)(2,1)S(1)}, bf16[512,256]{1,0:T(8,128)(2,1)S(1)}, u32[]{:S(2)}, u32[]{:S(2)}) collective-permute-start(bf16[512,256]{1,0:T(8,128)(2,1)S(1)} %add_convert_fusion.1), channel_id=1, source_target_pairs={{0,1},{1,0},{2,3},{3,2},{4,5},{5,4},{6,7},{7,6},{8,9},{9,8},{10,11... | collective-permute-start | bytes 786440 | tf_op jit(solution)/shard_map/ppermute | solution.py:22
  192.5 14.8 %collective-permute-start.14 = (bf16[512,256]{1,0:T(8,128)(2,1)S(1)}, bf16[512,256]{1,0:T(8,128)(2,1)S(1)}, u32[]{:S(2)}, u32[]{:S(2)}) collective-permute-start(bf16[512,256]{1,0:T(8,128)(2,1)S(1)} %add_convert_fusion.1), channel_id=1, source_target_pairs={{0,2},{1,3},{2,0},{3,1},{4,6},{5,7},{6,4},{7,5},{8,10},{9,11},{10,... | collective-permute-start | bytes 786440 | tf_op jit(solution)/shard_map/ppermute | solution.py:22
  193.9 13.3 %collective-permute-start.15 = (bf16[512,256]{1,0:T(8,128)(2,1)S(1)}, bf16[512,256]{1,0:T(8,128)(2,1)S(1)}, u32[]{:S(2)}, u32[]{:S(2)}) collective-permute-start(bf16[512,256]{1,0:T(8,128)(2,1)S(1)} %add_convert_fusion.1), channel_id=1, source_target_pairs={{0,3},{1,2},{2,1},{3,0},{4,7},{5,6},{6,5},{7,4},{8,11},{9,10},{10,... | collective-permute-start | bytes 786440 | tf_op jit(solution)/shard_map/ppermute | solution.py:22
  194.5 18.5 %collective-permute-start.12 = (bf16[512,256]{1,0:T(8,128)(2,1)}, bf16[512,256]{1,0:T(8,128)(2,1)}, u32[]{:S(2)}, u32[]{:S(2)}) collective-permute-start(bf16[512,256]{1,0:T(8,128)(2,1)} %get-tuple-element.44), channel_id=1, source_target_pairs={{0,2},{1,3},{2,0},{3,1},{4,6},{5,7},{6,4},{7,5},{8,10},{9,11},{10,... | collective-permute-start | bytes 786440 | tf_op jit(solution)/shard_map/ppermute | solution.py:22
  196.0 18.4 %collective-permute-start.8 = (bf16[512,256]{1,0:T(8,128)(2,1)}, bf16[512,256]{1,0:T(8,128)(2,1)}, u32[]{:S(2)}, u32[]{:S(2)}) collective-permute-start(bf16[512,256]{1,0:T(8,128)(2,1)} %get-tuple-element.40), channel_id=1, source_target_pairs={{0,1},{1,0},{2,3},{3,2},{4,5},{5,4},{6,7},{7,6},{8,9},{9,8},{10,11... | collective-permute-start | bytes 786440 | tf_op jit(solution)/shard_map/ppermute | solution.py:22
  200.1 18.5 %collective-permute-start.11 = (bf16[512,256]{1,0:T(8,128)(2,1)}, bf16[512,256]{1,0:T(8,128)(2,1)}, u32[]{:S(2)}, u32[]{:S(2)}) collective-permute-start(bf16[512,256]{1,0:T(8,128)(2,1)} %get-tuple-element.43), channel_id=1, source_target_pairs={{0,2},{1,3},{2,0},{3,1},{4,6},{5,7},{6,4},{7,5},{8,10},{9,11},{10,... | collective-permute-start | bytes 786440 | tf_op jit(solution)/shard_map/ppermute | solution.py:22
  208.7 9.9 %copy-start.26 = (bf16[512,256]{1,0:T(8,128)(2,1)S(1)}, bf16[512,256]{1,0:T(8,128)(2,1)}, u32[]{:S(2)}) copy-start(bf16[512,256]{1,0:T(8,128)(2,1)} %copy-done.25) | copy-start | bytes 786436
  210.8 9.5 %collective-permute-start.7 = (bf16[512,256]{1,0:T(8,128)(2,1)}, bf16[512,256]{1,0:T(8,128)(2,1)S(1)}, u32[]{:S(2)}, u32[]{:S(2)}) collective-permute-start(bf16[512,256]{1,0:T(8,128)(2,1)} %get-tuple-element.39), channel_id=1, source_target_pairs={{0,1},{1,0},{2,3},{3,2},{4,5},{5,4},{6,7},{7,6},{8,9},{9,8},{10,11... | collective-permute-start | bytes 786440 | tf_op jit(solution)/shard_map/ppermute | solution.py:22
  211.8 12.3 %collective-permute-start.10 = (bf16[512,256]{1,0:T(8,128)(2,1)}, bf16[512,256]{1,0:T(8,128)(2,1)S(1)}, u32[]{:S(2)}, u32[]{:S(2)}) collective-permute-start(bf16[512,256]{1,0:T(8,128)(2,1)} %get-tuple-element.42), channel_id=1, source_target_pairs={{0,2},{1,3},{2,0},{3,1},{4,6},{5,7},{6,4},{7,5},{8,10},{9,11},{10,... | collective-permute-start | bytes 786440 | tf_op jit(solution)/shard_map/ppermute | solution.py:22
  213.0 13.0 %collective-permute-start.6 = (bf16[512,256]{1,0:T(8,128)(2,1)}, bf16[512,256]{1,0:T(8,128)(2,1)S(1)}, u32[]{:S(2)}, u32[]{:S(2)}) collective-permute-start(bf16[512,256]{1,0:T(8,128)(2,1)} %get-tuple-element.38), channel_id=1, source_target_pairs={{0,1},{1,0},{2,3},{3,2},{4,5},{5,4},{6,7},{7,6},{8,9},{9,8},{10,11... | collective-permute-start | bytes 786440 | tf_op jit(solution)/shard_map/ppermute | solution.py:22
  214.4 14.4 %collective-permute-start.5 = (bf16[512,256]{1,0:T(8,128)(2,1)}, bf16[512,256]{1,0:T(8,128)(2,1)S(1)}, u32[]{:S(2)}, u32[]{:S(2)}) collective-permute-start(bf16[512,256]{1,0:T(8,128)(2,1)} %get-tuple-element.37), channel_id=1, source_target_pairs={{0,1},{1,0},{2,3},{3,2},{4,5},{5,4},{6,7},{7,6},{8,9},{9,8},{10,11... | collective-permute-start | bytes 786440 | tf_op jit(solution)/shard_map/ppermute | solution.py:22
  218.6 10.2 %collective-permute-start.9 = (bf16[512,256]{1,0:T(8,128)(2,1)S(1)}, bf16[512,256]{1,0:T(8,128)(2,1)S(1)}, u32[]{:S(2)}, u32[]{:S(2)}) collective-permute-start(bf16[512,256]{1,0:T(8,128)(2,1)S(1)} %copy-done.26), channel_id=1, source_target_pairs={{0,2},{1,3},{2,0},{3,1},{4,6},{5,7},{6,4},{7,5},{8,10},{9,11},{10,... | collective-permute-start | bytes 786440 | tf_op jit(solution)/shard_map/ppermute | solution.py:22
  (22 other events, 24.9 us)
Sparse Core Ops, SparseCore 0:
  10.2 43.5 all-gather.10
  55.4 36.7 all-gather.8
  93.8 37.1 all-gather.6
  132.4 37.1 all-gather.4
  171.8 39.1 reduce-scatter.7
  213.2 39.4 reduce-scatter.9
  254.9 39.4 reduce-scatter.11
  296.6 39.4 reduce-scatter.13
  338.9 30.0 reduce-scatter.15

commit v2 on v1

--- a/solution.py
+++ b/solution.py
@@ -15,6 +15,8 @@
 INV_ROOT_TWO_PI = 0.3989422804014327
 BF16 = jnp.bfloat16
 F32 = jnp.float32
+GATHER_LINES = (0, 1, 3)
+SCATTER_LINES = (2, 3)
 
 
 def swapped(block, axis, mask):
@@ -39,15 +41,62 @@
     return lax.dot_general(a, b, (((1,), (1,)), ((), ())), preferred_element_type=F32)
 
 
-def chunk_kernel(factors, local, aliased, *refs):
+def core_swap(x):
+    return swapped(x, "dp", 1)
+
+
+def moved(x, shift, sources):
+    pairs = [(2 * p + c, 2 * (p + shift) + c) for p in sources for c in range(2)]
+    return lax.ppermute(x, "dp", pairs)
+
+
+def line_gather(x):
+    chips = lax.axis_size("dp") // 2
+    chip = lax.axis_index("dp") // 2
+    from_left, from_right = [x], [x]
+    for step in range(1, chips):
+        from_left.append(moved(from_left[-1], 1, range(step - 1, chips - 1)))
+        from_right.append(moved(from_right[-1], -1, range(1, chips - step + 1)))
+    slots = [x] + [
+        jnp.where(chip >= j, from_left[j], from_right[chips - j]) for j in range(1, chips)
+    ]
+    own = jnp.stack(slots)
+    return own, core_swap(own)
+
+
+def line_scatter(mine, theirs):
+    chips = lax.axis_size("dp") // 2
+    chip = lax.axis_index("dp") // 2
+    pair = (mine.astype(F32) + core_swap(theirs).astype(F32)).astype(BF16)
+    pick = lambda index: lax.dynamic_index_in_dim(
+        pair, jnp.clip(index, 0, chips - 1), 0, keepdims=False
+    ).astype(F32)
+    right = left = None
+    for step in range(1, chips):
+        going_right, going_left = pick(chip + chips - step), pick(chip - chips + step)
+        if right is not None:
+            going_right = going_right + right.astype(F32)
+            going_left = going_left + left.astype(F32)
+        right = moved(going_right.astype(BF16), 1, range(0, step))
+        left = moved(going_left.astype(BF16), -1, range(chips - step, chips))
+    return (pick(chip) + right.astype(F32) + left.astype(F32)).astype(BF16)
+
+
+def chunk_kernel(factors, local, aliased, line_in, line_out, place_ref, *refs):
     pieces = refs[:factors]
-    cot_ref, w_ref = refs[factors:factors + 2]
-    rest = refs[factors + 2 + (1 if aliased else 0):]
-    hidden_ref, dw_ref, loc_ref = rest[:3]
-    far_refs = rest[3:3 + factors - 1 - local]
-    low_ref = rest[3 + factors - 1 - local]
-    x, xt, acc = rest[-3:]
+    cot_ref = refs[factors]
+    w_refs = refs[factors + 1:factors + 2 + line_in]
+    rest = refs[factors + 2 + line_in + aliased:]
+    hidden_ref = rest[0]
+    dw_refs = rest[1:2 + line_out]
+    loc_ref = rest[2 + line_out]
+    far_refs = rest[3 + line_out:3 + line_out + factors - 1 - local]
+    low_ref = rest[2 + line_out + factors - local]
+    x, xt, acc, wide = rest[-4:]
     step = pl.program_id(0)
+    chip, core = place_ref[0], place_ref[1]
+    chips, share = wide.shape[1], wide.shape[3]
+    depth = factors * BLK
 
     @pl.when(step == 0)
     def _():
@@ -56,12 +105,19 @@
             x[:, k * BLK:(k + 1) * BLK] = piece
             xt[k * BLK:(k + 1) * BLK, :] = piece.T
 
-    w = w_ref[0]
+    if line_in:
+        for s in range(chips):
+            slot = lax.rem(chip - s + chips, chips)
+            for k in range(factors):
+                wide[k, s, core] = w_refs[0][slot, 0, k]
+                wide[k, s, 1 - core] = w_refs[1][slot, 0, k]
+        w = wide[...].reshape(depth, BLK)
+    else:
+        w = w_refs[0][0]
     preact = jnp.dot(x[...], w, preferred_element_type=F32)
     act, slope = gelu_pair(preact)
     hidden_ref[...] = act.astype(BF16)
     grad = (cot_ref[...].astype(F32) * slope).astype(BF16)
-    dw_ref[0] = jnp.dot(xt[...], grad, preferred_element_type=F32).astype(BF16)
     back = nt_dot(grad, w)
 
     @pl.when(step == 0)
@@ -71,6 +127,16 @@
     @pl.when(step > 0)
     def _():
         acc[...] += back
+
+    dw = jnp.dot(xt[...], grad, preferred_element_type=F32).astype(BF16)
+    if line_out:
+        wide[...] = dw.reshape(wide.shape)
+        for s in range(chips):
+            for k in range(factors):
+                dw_refs[0][s, 0, k] = wide[k, s, core]
+                dw_refs[1][s, 0, k] = wide[k, s, 1 - core]
+    else:
+        dw_refs[0][0] = dw
 
     @pl.when(step == pl.num_programs(0) - 1)
     def _():
@@ -80,36 +146,39 @@
         low_ref[...] = acc[:, (factors - 1) * BLK:]
 
 
-def run_chunk(q, ratio, local, piece_arrays, piece_cols, cot, w, hidden_prev):
+def run_chunk(q, ratio, local, piece_arrays, piece_cols, cot, weights, hidden_prev, chips, line_out):
     rows, wide = cot.shape
     factors = len(piece_arrays)
     depth = factors * BLK
+    share = BLK // (2 * chips)
     n_far = factors - 1 - local
+    line_in = len(weights) == 2
+    place = jnp.stack([lax.axis_index("dp") // 2, lax.axis_index("dp") % 2])
     column = lambda col: pl.BlockSpec((rows, BLK), lambda h: (0, col))
-    in_specs = [column(col) for col in piece_cols]
-    in_specs += [
-        pl.BlockSpec((rows, BLK), lambda h: (0, q * ratio + h)),
-        pl.BlockSpec((1, depth, BLK), lambda h: (h, 0, 0)),
-    ]
-    args = list(piece_arrays) + [cot, w]
+    plain = pl.BlockSpec((1, depth, BLK), lambda h: (h, 0, 0))
+    lined = pl.BlockSpec((chips, 1, factors, share, BLK), lambda h: (0, h, 0, 0, 0))
+    in_specs = [pl.BlockSpec(memory_space=pltpu.SMEM)]
+    in_specs += [column(col) for col in piece_cols]
+    in_specs += [pl.BlockSpec((rows, BLK), lambda h: (0, q * ratio + h))]
+    in_specs += [lined, lined] if line_in else [plain]
+    args = [place] + list(piece_arrays) + [cot] + list(weights)
     aliases = {}
     if hidden_prev is not None:
         aliases = {len(args): 0}
         args.append(hidden_prev)
         in_specs.append(pl.BlockSpec(memory_space=pl.ANY))
     whole = lambda cols: pl.BlockSpec((rows, cols), lambda h: (0, 0))
-    out_specs = [
-        pl.BlockSpec((rows, BLK), lambda h: (0, q * ratio + h)),
-        pl.BlockSpec((1, depth, BLK), lambda h: (h, 0, 0)),
-        whole(local * BLK),
-    ] + [whole(BLK)] * (n_far + 1)
-    out_shape = [
-        jax.ShapeDtypeStruct((rows, wide), BF16),
-        jax.ShapeDtypeStruct((ratio, depth, BLK), BF16),
-        jax.ShapeDtypeStruct((rows, local * BLK), F32),
-    ] + [jax.ShapeDtypeStruct((rows, BLK), BF16)] * n_far + [jax.ShapeDtypeStruct((rows, BLK), F32)]
-    return pl.pallas_call(
-        functools.partial(chunk_kernel, factors, local, hidden_prev is not None),
+    out_specs = [pl.BlockSpec((rows, BLK), lambda h: (0, q * ratio + h))]
+    out_specs += [lined, lined] if line_out else [plain]
+    out_specs += [whole(local * BLK)] + [whole(BLK)] * (n_far + 1)
+    lined_shape = jax.ShapeDtypeStruct((chips, ratio, factors, share, BLK), BF16)
+    out_shape = [jax.ShapeDtypeStruct((rows, wide), BF16)]
+    out_shape += [lined_shape] * 2 if line_out else [jax.ShapeDtypeStruct((ratio, depth, BLK), BF16)]
+    out_shape += [jax.ShapeDtypeStruct((rows, local * BLK), F32)]
+    out_shape += [jax.ShapeDtypeStruct((rows, BLK), BF16)] * n_far
+    out_shape += [jax.ShapeDtypeStruct((rows, BLK), F32)]
+    outs = pl.pallas_call(
+        functools.partial(chunk_kernel, factors, local, int(hidden_prev is not None), int(line_in), int(line_out)),
         grid=(ratio,),
         in_specs=in_specs,
         out_specs=out_specs,
@@ -118,6 +187,7 @@
             pltpu.VMEM((rows, depth), BF16),
             pltpu.VMEM((depth, rows), BF16),
             pltpu.VMEM((rows, depth), F32),
+            pltpu.VMEM((factors, chips, 2, share, BLK), BF16),
         ],
         input_output_aliases=aliases,
         cost_estimate=pl.CostEstimate(
@@ -129,6 +199,8 @@
             dimension_semantics=("arbitrary",), vmem_limit_bytes=40 * 1024 * 1024
         ),
     )(*args)
+    dw = outs[1:2 + int(line_out)]
+    return outs[0], dw, outs[2 + int(line_out)], outs[3 + int(line_out):]
 
 
 def final_kernel(blocks, local_masks, n_far, *refs):
@@ -154,14 +226,21 @@
     far_masks = [(1 << b) // blocks for b in range(LOG) if 1 << b >= blocks]
     n_far = len(far_masks)
     factors = LOG + 2
+    chips = lax.axis_size("dp") // 2
+    short = chips <= 4 and blocks >= 4 and share % 16 == 0
+    gather_lines = GATHER_LINES if short else ()
+    scatter_lines = SCATTER_LINES if short else ()
 
     right_blocks = right_factor.reshape(share, hidden_blocks, BLK).transpose(1, 0, 2)
     weights = []
     for q in range(blocks):
         part = slice(q * ratio, (q + 1) * ratio)
         local_w = jnp.concatenate([butterfly[part], right_blocks[part][:, None]], axis=1)
-        full = lax.all_gather(local_w, "dp", axis=2, tiled=True)
-        weights.append(full.reshape(ratio, factors * BLK, BLK))
+        if q in gather_lines:
+            weights.append(line_gather(local_w))
+        else:
+            full = lax.all_gather(local_w, "dp", axis=2, tiled=True)
+            weights.append((full.reshape(ratio, factors * BLK, BLK),))
 
     left_full = lax.all_gather(left_factor, "dp", axis=0, tiled=True)
     far_tokens = [swapped(tokens, "tensor", mask) for mask in far_masks]
@@ -173,14 +252,18 @@
     for q in range(blocks):
         arrays = [tokens] * len(local_masks) + far_tokens + [low]
         columns = [q ^ mask for mask in local_masks] + [q] * n_far + [0]
-        hidden, dw, loc, *more = run_chunk(
-            q, ratio, len(local_masks), arrays, columns, cotangent, weights[q], hidden
+        hidden, dw, loc, more = run_chunk(
+            q, ratio, len(local_masks), arrays, columns, cotangent, weights[q], hidden,
+            chips, q in scatter_lines,
         )
-        grads.append(
-            lax.psum_scatter(
-                dw.reshape(ratio, factors, BLK, BLK), "dp", scatter_dimension=2, tiled=True
+        if q in scatter_lines:
+            grads.append(line_scatter(*dw))
+        else:
+            grads.append(
+                lax.psum_scatter(
+                    dw[0].reshape(ratio, factors, BLK, BLK), "dp", scatter_dimension=2, tiled=True
+                )
             )
-        )
         locs.append(loc)
         for i, mask in enumerate(far_masks):
             fars[i].append(swapped(more[i], "tensor", mask))
@@ -188,7 +271,15 @@
 
     grad_low = summed_over(low_back.astype(BF16), "tensor")
     grad_first = jnp.einsum("td,tr->dr", tokens, grad_low, preferred_element_type=F32)
-    sum_first = lax.psum_scatter(grad_first.astype(BF16), "dp", scatter_dimension=0, tiled=True)
+    grad_first = grad_first.astype(BF16)
+    if short:
+        by_owner = grad_first.reshape(chips, 2, -1, BLK)
+        core = lax.axis_index("dp") % 2
+        mine = lax.dynamic_index_in_dim(by_owner, core, 1, keepdims=False)
+        theirs = lax.dynamic_index_in_dim(by_owner, 1 - core, 1, keepdims=False)
+        sum_first = line_scatter(mine, theirs)
+    else:
+        sum_first = lax.psum_scatter(grad_first, "dp", scatter_dimension=0, tiled=True)
     grad_tokens = pl.pallas_call(
         functools.partial(final_kernel, blocks, local_masks, n_far),
         out_shape=jax.ShapeDtypeStruct(tokens.shape, BF16),

time: 377 us -> 417 us (1.11)
  starting transfers between devices: 22.2 us -> 80.9 us
  waiting for transfers between devices: 219 us -> 192 us
  other arithmetic: 5.08 us -> 16.7 us
  local copies, waits for them, and re-layouts: 40.6 us -> 33.8 us
  Pallas kernels: 55.8 us -> 61.2 us
    ppermute x0 -> x36, waiting for transfers between devices: none -> 159 us  [moved(): return lax.ppermute(x, 'dp', pairs)]
    reduce_scatter x4 -> x2, waiting for transfers between devices: 97.1 us -> 0.04 us  [per_device(): lax.psum_scatter(dw[0].reshape(ratio, factors, BLK, BLK), 'dp', scatter_d...]
    ppermute x0 -> x36, starting transfers between devices: none -> 58.4 us  [moved(): return lax.ppermute(x, 'dp', pairs)]
    all_gather x4 -> x1, waiting for transfers between devices: 57.9 us -> 0.02 us  [per_device(): full = lax.all_gather(local_w, 'dp', axis=2, tiled=True)]
    unnamed x10 -> x3, waiting for transfers between devices: 30.1 us -> 0.05 us
    unnamed x63 -> x67, local copies, waits for them, and re-layouts: 36.2 us -> 23.2 us
    convert_element_type x0 -> x15, other arithmetic: none -> 7.47 us  [the longest x3 5.16 us: line_scatter(): pair = (mine.astype(F32) + core_swap(theirs).astype(F32)).astype(BF16)]
    pallas_call x4, Pallas kernels: 53 us -> 58 us  [run_chunk(): pl.pallas_call(functools.partial(chunk_kernel, factors, local, int(hidden...]
  transfers between devices with their start and end apart: 25 -> 61, of which waited for: 18 -> 26; matrix products, arithmetic and copies ran while one was open for 4% -> 6% of each run, Pallas kernels for 15% -> 15%
where the time goes in v2:
time: 417 us; the launch traced here: 416 us
  waiting for transfers between devices  192 us (46%)
  starting transfers between devices  80.9 us (19%)
  Pallas kernels  61.2 us (15%)
  local copies, waits for them, and re-layouts  33.8 us (8%)
  other arithmetic  16.7 us (4%)
  blocking collectives  14.9 us (4%)
  between operations  14.8 us (4%)
    ppermute x36, waiting for transfers between devices, moved(): return lax.ppermute(x, 'dp', pairs)  159 us
    ppermute x36, starting transfers between devices, moved(): return lax.ppermute(x, 'dp', pairs)  58.4 us
    pallas_call x4, Pallas kernels, run_chunk(): pl.pallas_call(functools.partial(chunk_kernel, factors, local, int(hidden...  58 us
    ppermute x22, waiting for transfers between devices, swapped(): return lax.ppermute(block, axis, [(i, i ^ mask) for i in range(count)])  32.7 us
    unnamed x67, local copies, waits for them, and re-layouts  23.2 us
    ppermute x22, starting transfers between devices, swapped(): return lax.ppermute(block, axis, [(i, i ^ mask) for i in range(count)])  22.4 us
    all_gather x1, blocking collectives, per_device(): left_full = lax.all_gather(left_factor, 'dp', axis=0, tiled=True)  14.9 us
  transfers between devices with their start and end apart: 61, of which 26 were waited for; matrix products, arithmetic and copies ran while one was open for 6% of the time, Pallas kernels for 15%

profile of v2, /device:TPU:0, one launch (start us, length us, event | category | flops | bytes accessed | tf_op | source)
XLA Modules:
  0.0 415.8 jit_solution(10577107530352122647)
XLA Ops:
  11.4 5.0 %collective-permute-start.19 = (bf16[4,6,32,256]{3,2,1,0:T(8,128)(2,1)S(1)}, bf16[4,6,32,256]{3,2,1,0:T(8,128)(2,1)S(1)}, u32[]{:S(2)}, u32[]{:S(2)}) collective-permute-start(bf16[4,6,32,256]{3,2,1,0:T(8,128)(2,1)S(1)} %get-tuple-element.72), channel_id=1, source_target_pairs={{0,8},{4,12},{8,16},{12,20},{16,24},{20,28},{1,9},{5,13},{9,17},{1... | collective-permute-start | bytes 1179656 | tf_op jit(solution)/shard_map/ppermute | solution.py:50
  17.7 10.5 %collective-permute-done.19 = bf16[4,6,32,256]{3,2,1,0:T(8,128)(2,1)S(1)} collective-permute-done((bf16[4,6,32,256]{3,2,1,0:T(8,128)(2,1)S(1)}, bf16[4,6,32,256]{3,2,1,0:T(8,128)(2,1)S(1)}, u32[]{:S(2)}, u32[]{:S(2)}) %collective-permute-start.19) | collective-permute-done | bytes 393248 | tf_op jit(solution)/shard_map/ppermute | solution.py:50
  28.8 11.7 %collective-permute-done.20 = bf16[4,6,32,256]{3,2,1,0:T(8,128)(2,1)S(1)} collective-permute-done((bf16[4,6,32,256]{3,2,1,0:T(8,128)(2,1)S(1)}, bf16[4,6,32,256]{3,2,1,0:T(8,128)(2,1)S(1)}, u32[]{:S(2)}, u32[]{:S(2)}) %collective-permute-start.20) | collective-permute-done | bytes 393248 | tf_op jit(solution)/shard_map/ppermute | solution.py:50
  42.5 20.0 %collective-permute-done.21 = bf16[4,6,32,256]{3,2,1,0:T(8,128)(2,1)S(1)} collective-permute-done((bf16[4,6,32,256]{3,2,1,0:T(8,128)(2,1)S(1)}, bf16[4,6,32,256]{3,2,1,0:T(8,128)(2,1)S(1)}, u32[]{:S(2)}, u32[]{:S(2)}) %collective-permute-start.21) | collective-permute-done | bytes 393248 | tf_op jit(solution)/shard_map/ppermute | solution.py:50
  63.9 9.5 %collective-permute-done.22 = bf16[4,6,32,256]{3,2,1,0:T(8,128)(2,1)S(1)} collective-permute-done((bf16[4,6,32,256]{3,2,1,0:T(8,128)(2,1)S(1)}, bf16[4,6,32,256]{3,2,1,0:T(8,128)(2,1)S(1)}, u32[]{:S(2)}, u32[]{:S(2)}) %collective-permute-start.22) | collective-permute-done | bytes 393248 | tf_op jit(solution)/shard_map/ppermute | solution.py:50
  77.9 14.9 %all_gather.6.refs_13_ = bf16[1024,256]{1,0:T(8,128)(2,1)S(1)} all-gather(bf16[128,256]{1,0:T(8,128)(2,1)S(1)} %copy-done.32), channel_id=1, replica_groups=mesh['dp'=8,'tensor'=4] {'dp'}, dimensions={0}, use_global_device_ids=true | all-gather | bytes 589824 | tf_op jit(solution)/shard_map/all_gather | solution.py:245
  95.4 10.9 %collective-permute-done.4 = bf16[512,256]{1,0:T(8,128)(2,1)S(1)} collective-permute-done((bf16[512,256]{1,0:T(8,128)(2,1)S(1)}, bf16[512,256]{1,0:T(8,128)(2,1)S(1)}, u32[]{:S(2)}, u32[]{:S(2)}) %collective-permute-start.4) | collective-permute-done | bytes 262176 | tf_op jit(solution)/shard_map/ppermute | solution.py:24
  116.2 14.6 %shard_map.92 = (bf16[512,4096]{1,0:T(8,128)(2,1)}, bf16[4,1536,256]{2,1,0:T(8,128)(2,1)}, f32[512,768]{1,0:T(8,128)S(1)}, bf16[512,256]{1,0:T(8,128)(2,1)}, bf1...) custom-call(s32[2]{0:T(128)S(1)} %pad_add_fusion.place_ref, bf16[512,1024]{1,0:T(8,128)(2,1)S(1)} %copy-done.12, ...), custom_call_target="tpu_custom_call" | custom-call | flops 4831838208 | bytes 12320768 | tf_op jit(solution)/shard_map/pallas_call | solution.py:180
  139.8 11.9 %collective-permute-done.12 = bf16[4,6,32,256]{3,2,1,0:T(8,128)(2,1)S(1)} collective-permute-done((bf16[4,6,32,256]{3,2,1,0:T(8,128)(2,1)S(1)}, bf16[4,6,32,256]{3,2,1,0:T(8,128)(2,1)S(1)}, u32[]{:S(2)}, u32[]{:S(2)}) %collective-permute-start.12) | collective-permute-done | bytes 393248 | tf_op jit(solution)/shard_map/ppermute | solution.py:50
  152.3 12.1 %collective-permute-done.5 = bf16[4,6,32,256]{3,2,1,0:T(8,128)(2,1)S(1)} collective-permute-done((bf16[4,6,32,256]{3,2,1,0:T(8,128)(2,1)S(1)}, bf16[4,6,32,256]{3,2,1,0:T(8,128)(2,1)S(1)}, u32[]{:S(2)}, u32[]{:S(2)}) %collective-permute-start.5) | collective-permute-done | bytes 393248 | tf_op jit(solution)/shard_map/ppermute | solution.py:50
  166.4 12.4 %collective-permute-done.13 = bf16[4,6,32,256]{3,2,1,0:T(8,128)(2,1)S(1)} collective-permute-done((bf16[4,6,32,256]{3,2,1,0:T(8,128)(2,1)S(1)}, bf16[4,6,32,256]{3,2,1,0:T(8,128)(2,1)S(1)}, u32[]{:S(2)}, u32[]{:S(2)}) %collective-permute-start.13) | collective-permute-done | bytes 393248 | tf_op jit(solution)/shard_map/ppermute | solution.py:50
  181.6 12.5 %collective-permute-done.7 = bf16[4,6,32,256]{3,2,1,0:T(8,128)(2,1)S(1)} collective-permute-done((bf16[4,6,32,256]{3,2,1,0:T(8,128)(2,1)S(1)}, bf16[4,6,32,256]{3,2,1,0:T(8,128)(2,1)S(1)}, u32[]{:S(2)}, u32[]{:S(2)}) %collective-permute-start.7) | collective-permute-done | bytes 393248 | tf_op jit(solution)/shard_map/ppermute | solution.py:50
  195.4 7.1 %collective-permute-done.14 = bf16[4,6,32,256]{3,2,1,0:T(8,128)(2,1)S(1)} collective-permute-done((bf16[4,6,32,256]{3,2,1,0:T(8,128)(2,1)S(1)}, bf16[4,6,32,256]{3,2,1,0:T(8,128)(2,1)S(1)}, u32[]{:S(2)}, u32[]{:S(2)}) %collective-permute-start.14) | collective-permute-done | bytes 393248 | tf_op jit(solution)/shard_map/ppermute | solution.py:50
  204.1 14.3 %collective-permute-done.15 = bf16[4,6,32,256]{3,2,1,0:T(8,128)(2,1)S(1)} collective-permute-done((bf16[4,6,32,256]{3,2,1,0:T(8,128)(2,1)S(1)}, bf16[4,6,32,256]{3,2,1,0:T(8,128)(2,1)S(1)}, u32[]{:S(2)}, u32[]{:S(2)}) %collective-permute-start.15) | collective-permute-done | bytes 393248 | tf_op jit(solution)/shard_map/ppermute | solution.py:50
  222.2 14.5 %shard_map.93 = (bf16[512,4096]{1,0:T(8,128)(2,1)}, bf16[4,1536,256]{2,1,0:T(8,128)(2,1)}, f32[512,768]{1,0:T(8,128)S(1)}, bf16[512,256]{1,0:T(8,128)(2,1)}, bf1...) custom-call(s32[2]{0:T(128)S(1)} %pad_add_fusion.place_ref, ...), custom_call_target="tpu_custom_call", output_to_operand_aliasing={{0}: (10, {})} | custom-call | flops 4831838208 | bytes 12320768 | tf_op jit(solution)/shard_map/pallas_call | solution.py:180
  241.3 14.1 %shard_map.94 = (bf16[512,4096]{1,0:T(8,128)(2,1)}, bf16[4,4,6,32,256]{4,3,2,1,0:T(8,128)(2,1)S(1)}, bf16[4,4,6,32,256]{4,3,2,1,0:T(8,128)(2,1)S(1)}, f32[512,76...) custom-call(s32[2]{0:T(128)S(1)} %pad_add_fusion.place_ref, ...), custom_call_target="tpu_custom_call", output_to_operand_aliasing={{0}: (9, {})} | custom-call | flops 4831838208 | bytes 12320768 | tf_op jit(solution)/shard_map/pallas_call | solution.py:180
  260.4 14.8 %shard_map.95 = (bf16[512,4096]{1,0:T(8,128)(2,1)}, bf16[4,4,6,32,256]{4,3,2,1,0:T(8,128)(2,1)S(1)}, bf16[4,4,6,32,256]{4,3,2,1,0:T(8,128)(2,1)}, f32[512,768]{1...) custom-call(s32[2]{0:T(128)S(1)} %pad_add_fusion.place_ref, ...), custom_call_target="tpu_custom_call", output_to_operand_aliasing={{0}: (10, {})} | custom-call | flops 4831838208 | bytes 12320768 | tf_op jit(solution)/shard_map/pallas_call | solution.py:180
  283.2 5.1 %collective-permute-done.36 = bf16[512,256]{1,0:T(8,128)(2,1)S(1)} collective-permute-done((bf16[512,256]{1,0:T(8,128)(2,1)S(1)}, bf16[512,256]{1,0:T(8,128)(2,1)S(1)}, u32[]{:S(2)}, u32[]{:S(2)}) %collective-permute-start.36) | collective-permute-done | bytes 262176 | tf_op jit(solution)/shard_map/ppermute | solution.py:24
  289.8 3.4 collective-permute-done.35
  296.7 3.0 collective-permute-done.26.refs_4_
  301.7 3.6 collective-permute-done.27.refs_5_
  323.6 3.2 shard_map.96
  327.8 3.8 collective-permute-start.52
  341.4 3.9 collective-permute-done.45
  346.1 7.5 %collective-permute-done.38 = bf16[4,6,32,256]{3,2,1,0:T(8,128)(2,1)S(1)} collective-permute-done((bf16[4,6,32,256]{3,2,1,0:T(8,128)(2,1)S(1)}, bf16[4,6,32,256]{3,2,1,0:T(8,128)(2,1)S(1)}, u32[]{:S(2)}, u32[]{:S(2)}) %collective-permute-start.38) | collective-permute-done | bytes 393248 | tf_op jit(solution)/shard_map/ppermute | solution.py:50
  353.6 4.4 %collective-permute-start.46 = (bf16[4,6,32,256]{3,2,1,0:T(8,128)(2,1)S(1)}, bf16[4,6,32,256]{3,2,1,0:T(8,128)(2,1)S(1)}, u32[]{:S(2)}, u32[]{:S(2)}) collective-permute-start(bf16[4,6,32,256]{3,2,1,0:T(8,128)(2,1)S(1)} %fusion.3), channel_id=1, source_target_pairs={{0,8},{4,12},{8,16},{12,20},{1,9},{5,13},{9,17},{13,21},{2,10},{6,... | collective-permute-start | bytes 1179656 | tf_op jit(solution)/shard_map/ppermute | solution.py:50
  362.8 4.8 %collective-permute-done.46 = bf16[4,6,32,256]{3,2,1,0:T(8,128)(2,1)S(1)} collective-permute-done((bf16[4,6,32,256]{3,2,1,0:T(8,128)(2,1)S(1)}, bf16[4,6,32,256]{3,2,1,0:T(8,128)(2,1)S(1)}, u32[]{:S(2)}, u32[]{:S(2)}) %collective-permute-start.46) | collective-permute-done | bytes 393248 | tf_op jit(solution)/shard_map/ppermute | solution.py:50
  368.6 5.7 %collective-permute-done.39 = bf16[4,6,32,256]{3,2,1,0:T(8,128)(2,1)S(1)} collective-permute-done((bf16[4,6,32,256]{3,2,1,0:T(8,128)(2,1)S(1)}, bf16[4,6,32,256]{3,2,1,0:T(8,128)(2,1)S(1)}, u32[]{:S(2)}, u32[]{:S(2)}) %collective-permute-start.39) | collective-permute-done | bytes 393248 | tf_op jit(solution)/shard_map/ppermute | solution.py:50
  376.6 5.6 %collective-permute-start.47 = (bf16[4,6,32,256]{3,2,1,0:T(8,128)(2,1)S(1)}, bf16[4,6,32,256]{3,2,1,0:T(8,128)(2,1)S(1)}, u32[]{:S(2)}, u32[]{:S(2)}) collective-permute-start(bf16[4,6,32,256]{3,2,1,0:T(8,128)(2,1)S(1)} %get-tuple-element.61), channel_id=1, source_target_pairs={{0,8},{4,12},{8,16},{12,20},{16,24},{20,28},{1,9},{5,13},{9,17},{1... | collective-permute-start | bytes 1179656 | tf_op jit(solution)/shard_map/ppermute | solution.py:50
  382.3 4.6 %collective-permute-start.40 = (bf16[4,6,32,256]{3,2,1,0:T(8,128)(2,1)S(1)}, bf16[4,6,32,256]{3,2,1,0:T(8,128)(2,1)S(1)}, u32[]{:S(2)}, u32[]{:S(2)}) collective-permute-start(bf16[4,6,32,256]{3,2,1,0:T(8,128)(2,1)S(1)} %get-tuple-element.57), channel_id=1, source_target_pairs={{0,8},{4,12},{8,16},{12,20},{16,24},{20,28},{1,9},{5,13},{9,17},{1... | collective-permute-start | bytes 1179656 | tf_op jit(solution)/shard_map/ppermute | solution.py:50
  391.8 9.3 %collective-permute-done.50 = bf16[4,6,32,256]{3,2,1,0:T(8,128)(2,1)S(1)} collective-permute-done((bf16[4,6,32,256]{3,2,1,0:T(8,128)(2,1)S(1)}, bf16[4,6,32,256]{3,2,1,0:T(8,128)(2,1)S(1)}, u32[]{:S(2)}, u32[]{:S(2)}) %collective-permute-start.50) | collective-permute-done | bytes 393248 | tf_op jit(solution)/shard_map/ppermute | solution.py:50
  401.3 4.3 %collective-permute-done.43 = bf16[4,6,32,256]{3,2,1,0:T(8,128)(2,1)S(1)} collective-permute-done((bf16[4,6,32,256]{3,2,1,0:T(8,128)(2,1)S(1)}, bf16[4,6,32,256]{3,2,1,0:T(8,128)(2,1)S(1)}, u32[]{:S(2)}, u32[]{:S(2)}) %collective-permute-start.43) | collective-permute-done | bytes 393248 | tf_op jit(solution)/shard_map/ppermute | solution.py:50
  (216 shorter events, 118.0 us)
Async XLA Ops:
  7.2 232.2 %all-gather.2.cloned.1.call-start = ((), (), s32[]{:S(2)}) async-start(), calls=%async_computation.2 | async-start | bytes 3538944 | tf_op jit(solution)/shard_map/all_gather | solution.py:242
  11.3 394.5 %reduce-scatter.3.cloned.1.call-start = ((), (), s32[]{:S(2)}) async-start(), calls=%async_computation.3 | async-start | bytes 3538944 | tf_op jit(solution)/shard_map/reduce_scatter | solution.py:263
  11.4 16.7 %collective-permute-start.19 = (bf16[4,6,32,256]{3,2,1,0:T(8,128)(2,1)S(1)}, bf16[4,6,32,256]{3,2,1,0:T(8,128)(2,1)S(1)}, u32[]{:S(2)}, u32[]{:S(2)}) collective-permute-start(bf16[4,6,32,256]{3,2,1,0:T(8,128)(2,1)S(1)} %get-tuple-element.72), channel_id=1, source_target_pairs={{0,8},{4,12},{8,16},{12,20},{16,24},{20,28},{1,9},{5,13},{9,17},{1... | collective-permute-start | bytes 1179656 | tf_op jit(solution)/shard_map/ppermute | solution.py:50
  16.4 24.1 %collective-permute-start.20 = (bf16[4,6,32,256]{3,2,1,0:T(8,128)(2,1)S(1)}, bf16[4,6,32,256]{3,2,1,0:T(8,128)(2,1)S(1)}, u32[]{:S(2)}, u32[]{:S(2)}) collective-permute-start(bf16[4,6,32,256]{3,2,1,0:T(8,128)(2,1)S(1)} %get-tuple-element.72), channel_id=1, source_target_pairs={{8,0},{12,4},{16,8},{20,12},{24,16},{28,20},{9,1},{13,5},{17,9},{2... | collective-permute-start | bytes 1179656 | tf_op jit(solution)/shard_map/ppermute | solution.py:50
  40.5 22.0 %collective-permute-start.21 = (bf16[4,6,32,256]{3,2,1,0:T(8,128)(2,1)S(1)}, bf16[4,6,32,256]{3,2,1,0:T(8,128)(2,1)S(1)}, u32[]{:S(2)}, u32[]{:S(2)}) collective-permute-start(bf16[4,6,32,256]{3,2,1,0:T(8,128)(2,1)S(1)} %collective-permute-done.20), channel_id=1, source_target_pairs={{8,0},{12,4},{16,8},{20,12},{9,1},{13,5},{17,9},{21,13},{10,2},{14... | collective-permute-start | bytes 1179656 | tf_op jit(solution)/shard_map/ppermute | solution.py:50
  41.8 22.1 %collective-permute-start.24 = (bf16[4,6,32,256]{3,2,1,0:T(8,128)(2,1)S(1)}, bf16[4,6,32,256]{3,2,1,0:T(8,128)(2,1)S(1)}, u32[]{:S(2)}, u32[]{:S(2)}) collective-permute-start(bf16[4,6,32,256]{3,2,1,0:T(8,128)(2,1)S(1)} %collective-permute-done.23), channel_id=1, source_target_pairs={{16,24},{20,28},{17,25},{21,29},{18,26},{22,30},{19,27},{23,31}} | collective-permute-start | bytes 1179656 | tf_op jit(solution)/shard_map/ppermute | solution.py:50
  73.7 41.1 %collective-permute-start.25 = (bf16[4,4,6,32,256]{4,3,2,1,0:T(8,128)(2,1)S(1)}, bf16[4,4,6,32,256]{4,3,2,1,0:T(8,128)(2,1)}, u32[]{:S(2)}, u32[]{:S(2)}) collective-permute-start(bf16[4,4,6,32,256]{4,3,2,1,0:T(8,128)(2,1)S(1)} %pad_maximum_fusion.2.refs_7_), channel_id=1, source_target_pairs={{0,4},{4,0},{8,12},{12,8},{16,20},{20,16},{24,28},{28,24},{1,5},{5... | collective-permute-start | bytes 4718600 | tf_op jit(solution)/shard_map/ppermute | solution.py:24
  74.9 39.9 %collective-permute-start.1 = (bf16[512,1024]{1,0:T(8,128)(2,1)S(1)}, bf16[512,1024]{1,0:T(8,128)(2,1)}, u32[]{:S(2)}, u32[]{:S(2)}) collective-permute-start(bf16[512,1024]{1,0:T(8,128)(2,1)S(1)} %copy-done.12), channel_id=1, source_target_pairs={{0,2},{1,3},{2,0},{3,1},{4,6},{5,7},{6,4},{7,5},{8,10},{9,11},{10,... | collective-permute-start | bytes 3145736 | tf_op jit(solution)/shard_map/ppermute | solution.py:24
  76.4 38.4 %collective-permute-start = (bf16[512,1024]{1,0:T(8,128)(2,1)S(1)}, bf16[512,1024]{1,0:T(8,128)(2,1)}, u32[]{:S(2)}, u32[]{:S(2)}) collective-permute-start(bf16[512,1024]{1,0:T(8,128)(2,1)S(1)} %copy-done.12), channel_id=1, source_target_pairs={{0,1},{1,0},{2,3},{3,2},{4,5},{5,4},{6,7},{7,6},{8,9},{9,8},{10,11... | collective-permute-start | bytes 3145736 | tf_op jit(solution)/shard_map/ppermute | solution.py:24
  93.8 16.9 %collective-permute-start.3 = (bf16[512,256]{1,0:T(8,128)(2,1)S(1)}, bf16[512,256]{1,0:T(8,128)(2,1)}, u32[]{:S(2)}, u32[]{:S(2)}) collective-permute-start(bf16[512,256]{1,0:T(8,128)(2,1)S(1)} %convolution_convert_fusion.1), channel_id=1, source_target_pairs={{0,2},{1,3},{2,0},{3,1},{4,6},{5,7},{6,4},{7,5},{8,10},{9,11},{10,... | collective-permute-start | bytes 786440 | tf_op jit(solution)/shard_map/ppermute | solution.py:24
  131.6 274.2 %reduce-scatter.5.cloned.1.call-start = ((), (), s32[]{:S(2)}) async-start(), calls=%async_computation.4 | async-start | bytes 3538944 | tf_op jit(solution)/shard_map/reduce_scatter | solution.py:263
  132.7 18.9 %collective-permute-start.12 = (bf16[4,6,32,256]{3,2,1,0:T(8,128)(2,1)S(1)}, bf16[4,6,32,256]{3,2,1,0:T(8,128)(2,1)S(1)}, u32[]{:S(2)}, u32[]{:S(2)}) collective-permute-start(bf16[4,6,32,256]{3,2,1,0:T(8,128)(2,1)S(1)} %get-tuple-element.74), channel_id=1, source_target_pairs={{0,8},{4,12},{8,16},{12,20},{16,24},{20,28},{1,9},{5,13},{9,17},{1... | collective-permute-start | bytes 1179656 | tf_op jit(solution)/shard_map/ppermute | solution.py:50
  135.2 29.2 %collective-permute-start.5 = (bf16[4,6,32,256]{3,2,1,0:T(8,128)(2,1)S(1)}, bf16[4,6,32,256]{3,2,1,0:T(8,128)(2,1)S(1)}, u32[]{:S(2)}, u32[]{:S(2)}) collective-permute-start(bf16[4,6,32,256]{3,2,1,0:T(8,128)(2,1)S(1)} %get-tuple-element.76), channel_id=1, source_target_pairs={{0,8},{4,12},{8,16},{12,20},{16,24},{20,28},{1,9},{5,13},{9,17},{1... | collective-permute-start | bytes 1179656 | tf_op jit(solution)/shard_map/ppermute | solution.py:50
  137.2 28.0 %collective-permute-start.6 = (bf16[4,6,32,256]{3,2,1,0:T(8,128)(2,1)S(1)}, bf16[4,6,32,256]{3,2,1,0:T(8,128)(2,1)S(1)}, u32[]{:S(2)}, u32[]{:S(2)}) collective-permute-start(bf16[4,6,32,256]{3,2,1,0:T(8,128)(2,1)S(1)} %get-tuple-element.76), channel_id=1, source_target_pairs={{8,0},{12,4},{16,8},{20,12},{24,16},{28,20},{9,1},{13,5},{17,9},{2... | collective-permute-start | bytes 1179656 | tf_op jit(solution)/shard_map/ppermute | solution.py:50
  138.5 40.4 %collective-permute-start.13 = (bf16[4,6,32,256]{3,2,1,0:T(8,128)(2,1)S(1)}, bf16[4,6,32,256]{3,2,1,0:T(8,128)(2,1)S(1)}, u32[]{:S(2)}, u32[]{:S(2)}) collective-permute-start(bf16[4,6,32,256]{3,2,1,0:T(8,128)(2,1)S(1)} %get-tuple-element.74), channel_id=1, source_target_pairs={{8,0},{12,4},{16,8},{20,12},{24,16},{28,20},{9,1},{13,5},{17,9},{2... | collective-permute-start | bytes 1179656 | tf_op jit(solution)/shard_map/ppermute | solution.py:50
  151.6 28.5 %collective-permute-start.16 = (bf16[4,6,32,256]{3,2,1,0:T(8,128)(2,1)S(1)}, bf16[4,6,32,256]{3,2,1,0:T(8,128)(2,1)S(1)}, u32[]{:S(2)}, u32[]{:S(2)}) collective-permute-start(bf16[4,6,32,256]{3,2,1,0:T(8,128)(2,1)S(1)} %collective-permute-done.12), channel_id=1, source_target_pairs={{8,16},{12,20},{16,24},{20,28},{9,17},{13,21},{17,25},{21,29},{10,... | collective-permute-start | bytes 1179656 | tf_op jit(solution)/shard_map/ppermute | solution.py:50
  165.1 29.0 %collective-permute-start.7 = (bf16[4,6,32,256]{3,2,1,0:T(8,128)(2,1)S(1)}, bf16[4,6,32,256]{3,2,1,0:T(8,128)(2,1)S(1)}, u32[]{:S(2)}, u32[]{:S(2)}) collective-permute-start(bf16[4,6,32,256]{3,2,1,0:T(8,128)(2,1)S(1)} %collective-permute-done.6), channel_id=1, source_target_pairs={{8,0},{12,4},{16,8},{20,12},{9,1},{13,5},{17,9},{21,13},{10,2},{14... | collective-permute-start | bytes 1179656 | tf_op jit(solution)/shard_map/ppermute | solution.py:50
  178.9 23.7 %collective-permute-start.14 = (bf16[4,6,32,256]{3,2,1,0:T(8,128)(2,1)S(1)}, bf16[4,6,32,256]{3,2,1,0:T(8,128)(2,1)S(1)}, u32[]{:S(2)}, u32[]{:S(2)}) collective-permute-start(bf16[4,6,32,256]{3,2,1,0:T(8,128)(2,1)S(1)} %collective-permute-done.13), channel_id=1, source_target_pairs={{8,0},{12,4},{16,8},{20,12},{9,1},{13,5},{17,9},{21,13},{10,2},{14... | collective-permute-start | bytes 1179656 | tf_op jit(solution)/shard_map/ppermute | solution.py:50
  180.2 23.9 %collective-permute-start.17 = (bf16[4,6,32,256]{3,2,1,0:T(8,128)(2,1)S(1)}, bf16[4,6,32,256]{3,2,1,0:T(8,128)(2,1)S(1)}, u32[]{:S(2)}, u32[]{:S(2)}) collective-permute-start(bf16[4,6,32,256]{3,2,1,0:T(8,128)(2,1)S(1)} %collective-permute-done.16), channel_id=1, source_target_pairs={{16,24},{20,28},{17,25},{21,29},{18,26},{22,30},{19,27},{23,31}} | collective-permute-start | bytes 1179656 | tf_op jit(solution)/shard_map/ppermute | solution.py:50
  180.9 37.9 %collective-permute-start.10 = (bf16[4,6,32,256]{3,2,1,0:T(8,128)(2,1)S(1)}, bf16[4,6,32,256]{3,2,1,0:T(8,128)(2,1)S(1)}, u32[]{:S(2)}, u32[]{:S(2)}) collective-permute-start(bf16[4,6,32,256]{3,2,1,0:T(8,128)(2,1)S(1)} %collective-permute-done.9), channel_id=1, source_target_pairs={{16,24},{20,28},{17,25},{21,29},{18,26},{22,30},{19,27},{23,31}} | collective-permute-start | bytes 1179656 | tf_op jit(solution)/shard_map/ppermute | solution.py:50
  194.1 24.8 %collective-permute-start.8 = (bf16[4,6,32,256]{3,2,1,0:T(8,128)(2,1)S(1)}, bf16[4,6,32,256]{3,2,1,0:T(8,128)(2,1)S(1)}, u32[]{:S(2)}, u32[]{:S(2)}) collective-permute-start(bf16[4,6,32,256]{3,2,1,0:T(8,128)(2,1)S(1)} %collective-permute-done.7), channel_id=1, source_target_pairs={{8,0},{12,4},{9,1},{13,5},{10,2},{14,6},{11,3},{15,7}} | collective-permute-start | bytes 1179656 | tf_op jit(solution)/shard_map/ppermute | solution.py:50
  220.3 40.1 %collective-permute-start.11 = (bf16[4,4,6,32,256]{4,3,2,1,0:T(8,128)(2,1)}, bf16[4,4,6,32,256]{4,3,2,1,0:T(8,128)(2,1)}, u32[]{:S(2)}, u32[]{:S(2)}) collective-permute-start(bf16[4,4,6,32,256]{4,3,2,1,0:T(8,128)(2,1)} %pad_maximum_fusion.refs_7_), channel_id=1, source_target_pairs={{0,4},{4,0},{8,12},{12,8},{16,20},{20,16},{24,28},{28,24},{1,5},{5... | collective-permute-start | bytes 4718600 | tf_op jit(solution)/shard_map/ppermute | solution.py:24
  277.5 54.7 %collective-permute-start.44 = (bf16[4,4,6,32,256]{4,3,2,1,0:T(8,128)(2,1)}, bf16[4,4,6,32,256]{4,3,2,1,0:T(8,128)(2,1)}, u32[]{:S(2)}, u32[]{:S(2)}) collective-permute-start(bf16[4,4,6,32,256]{4,3,2,1,0:T(8,128)(2,1)} %get-tuple-element.56), channel_id=1, source_target_pairs={{0,4},{4,0},{8,12},{12,8},{16,20},{20,16},{24,28},{28,24},{1,5},{5... | collective-permute-start | bytes 4718600 | tf_op jit(solution)/shard_map/ppermute | solution.py:24
  281.7 18.0 %collective-permute-start.26 = (bf16[512,256]{1,0:T(8,128)(2,1)}, bf16[512,256]{1,0:T(8,128)(2,1)}, u32[]{:S(2)}, u32[]{:S(2)}) collective-permute-start(bf16[512,256]{1,0:T(8,128)(2,1)} %get-tuple-element.39), channel_id=1, source_target_pairs={{0,1},{1,0},{2,3},{3,2},{4,5},{5,4},{6,7},{7,6},{8,9},{9,8},{10,11... | collective-permute-start | bytes 786440 | tf_op jit(solution)/shard_map/ppermute | solution.py:24
  295.4 40.5 %collective-permute-start.37 = (bf16[4,4,6,32,256]{4,3,2,1,0:T(8,128)(2,1)}, bf16[4,4,6,32,256]{4,3,2,1,0:T(8,128)(2,1)}, u32[]{:S(2)}, u32[]{:S(2)}) collective-permute-start(bf16[4,4,6,32,256]{4,3,2,1,0:T(8,128)(2,1)} %copy-done.18), channel_id=1, source_target_pairs={{0,4},{4,0},{8,12},{12,8},{16,20},{20,16},{24,28},{28,24},{1,5},{5... | collective-permute-start | bytes 4718600 | tf_op jit(solution)/shard_map/ppermute | solution.py:24
  331.6 26.6 %collective-permute-start.55 = (bf16[128,256]{1,0:T(8,128)(2,1)S(1)}, bf16[128,256]{1,0:T(8,128)(2,1)S(1)}, u32[]{:S(2)}, u32[]{:S(2)}) collective-permute-start(bf16[128,256]{1,0:T(8,128)(2,1)S(1)} %get-tuple-element.80), channel_id=1, source_target_pairs={{24,16},{28,20},{25,17},{29,21},{26,18},{30,22},{27,19},{31,23}} | collective-permute-start | bytes 196616 | tf_op jit(solution)/shard_map/ppermute | solution.py:50
  339.4 20.7 %collective-permute-start.53 = (bf16[128,256]{1,0:T(8,128)(2,1)S(1)}, bf16[128,256]{1,0:T(8,128)(2,1)S(1)}, u32[]{:S(2)}, u32[]{:S(2)}) collective-permute-start(bf16[128,256]{1,0:T(8,128)(2,1)S(1)} %fusion.16), channel_id=1, source_target_pairs={{0,8},{4,12},{8,16},{12,20},{1,9},{5,13},{9,17},{13,21},{2,10},{6,... | collective-permute-start | bytes 196616 | tf_op jit(solution)/shard_map/ppermute | solution.py:50
  340.7 21.4 %collective-permute-start.48 = (bf16[4,6,32,256]{3,2,1,0:T(8,128)(2,1)S(1)}, bf16[4,6,32,256]{3,2,1,0:T(8,128)(2,1)S(1)}, u32[]{:S(2)}, u32[]{:S(2)}) collective-permute-start(bf16[4,6,32,256]{3,2,1,0:T(8,128)(2,1)S(1)} %get-tuple-element.64), channel_id=1, source_target_pairs={{24,16},{28,20},{25,17},{29,21},{26,18},{30,22},{27,19},{31,23}} | collective-permute-start | bytes 1179656 | tf_op jit(solution)/shard_map/ppermute | solution.py:50
  345.3 23.3 %collective-permute-start.41 = (bf16[4,6,32,256]{3,2,1,0:T(8,128)(2,1)S(1)}, bf16[4,6,32,256]{3,2,1,0:T(8,128)(2,1)S(1)}, u32[]{:S(2)}, u32[]{:S(2)}) collective-permute-start(bf16[4,6,32,256]{3,2,1,0:T(8,128)(2,1)S(1)} %get-tuple-element.60), channel_id=1, source_target_pairs={{24,16},{28,20},{25,17},{29,21},{26,18},{30,22},{27,19},{31,23}} | collective-permute-start | bytes 1179656 | tf_op jit(solution)/shard_map/ppermute | solution.py:50
  360.2 28.3 %collective-permute-start.54 = (bf16[128,256]{1,0:T(8,128)(2,1)S(1)}, bf16[128,256]{1,0:T(8,128)(2,1)S(1)}, u32[]{:S(2)}, u32[]{:S(2)}) collective-permute-start(bf16[128,256]{1,0:T(8,128)(2,1)S(1)} %get-tuple-element.77), channel_id=1, source_target_pairs={{0,8},{4,12},{8,16},{12,20},{16,24},{20,28},{1,9},{5,13},{9,17},{1... | collective-permute-start | bytes 196616 | tf_op jit(solution)/shard_map/ppermute | solution.py:50
  382.3 19.0 %collective-permute-start.40 = (bf16[4,6,32,256]{3,2,1,0:T(8,128)(2,1)S(1)}, bf16[4,6,32,256]{3,2,1,0:T(8,128)(2,1)S(1)}, u32[]{:S(2)}, u32[]{:S(2)}) collective-permute-start(bf16[4,6,32,256]{3,2,1,0:T(8,128)(2,1)S(1)} %get-tuple-element.57), channel_id=1, source_target_pairs={{0,8},{4,12},{8,16},{12,20},{16,24},{20,28},{1,9},{5,13},{9,17},{1... | collective-permute-start | bytes 1179656 | tf_op jit(solution)/shard_map/ppermute | solution.py:50
  388.5 17.1 %collective-permute-start.43 = (bf16[4,6,32,256]{3,2,1,0:T(8,128)(2,1)S(1)}, bf16[4,6,32,256]{3,2,1,0:T(8,128)(2,1)S(1)}, u32[]{:S(2)}, u32[]{:S(2)}) collective-permute-start(bf16[4,6,32,256]{3,2,1,0:T(8,128)(2,1)S(1)} %fusion.8), channel_id=1, source_target_pairs={{8,0},{12,4},{16,8},{20,12},{24,16},{28,20},{9,1},{13,5},{17,9},{2... | collective-permute-start | bytes 1179656 | tf_op jit(solution)/shard_map/ppermute | solution.py:50
  (62 other events, 512.2 us)
Sparse Core Ops, SparseCore 0:
  11.4 51.8 all-gather.1
  131.7 59.1 reduce-scatter.2
  239.5 38.4 reduce-scatter.4

commit v3 on v1

--- a/solution.py
+++ b/solution.py
@@ -39,10 +39,37 @@
     return lax.dot_general(a, b, (((1,), (1,)), ((), ())), preferred_element_type=F32)
 
 
+def core_swap(x):
+    return swapped(x, "dp", 1)
+
+
+def moved(x, shift, sources):
+    pairs = [(2 * p + c, 2 * (p + shift) + c) for p in sources for c in range(2)]
+    return lax.ppermute(x, "dp", pairs)
+
+
+def line_scatter(mine, theirs):
+    chips = lax.axis_size("dp") // 2
+    chip = lax.axis_index("dp") // 2
+    pair = (mine.astype(F32) + core_swap(theirs).astype(F32)).astype(BF16)
+    pick = lambda index: lax.dynamic_index_in_dim(
+        pair, jnp.clip(index, 0, chips - 1), 0, keepdims=False
+    ).astype(F32)
+    right = left = None
+    for step in range(1, chips):
+        going_right, going_left = pick(chip + chips - step), pick(chip - chips + step)
+        if right is not None:
+            going_right = going_right + right.astype(F32)
+            going_left = going_left + left.astype(F32)
+        right = moved(going_right.astype(BF16), 1, range(0, step))
+        left = moved(going_left.astype(BF16), -1, range(chips - step, chips))
+    return (pick(chip) + right.astype(F32) + left.astype(F32)).astype(BF16)
+
+
 def chunk_kernel(factors, local, aliased, *refs):
     pieces = refs[:factors]
     cot_ref, w_ref = refs[factors:factors + 2]
-    rest = refs[factors + 2 + (1 if aliased else 0):]
+    rest = refs[factors + 2 + aliased:]
     hidden_ref, dw_ref, loc_ref = rest[:3]
     far_refs = rest[3:3 + factors - 1 - local]
     low_ref = rest[3 + factors - 1 - local]
@@ -80,7 +107,7 @@
         low_ref[...] = acc[:, (factors - 1) * BLK:]
 
 
-def run_chunk(q, ratio, local, piece_arrays, piece_cols, cot, w, hidden_prev):
+def run_chunk(q, at, ratio, local, piece_arrays, piece_cols, cot, w, hidden_prev, dw_prev):
     rows, wide = cot.shape
     factors = len(piece_arrays)
     depth = factors * BLK
@@ -89,27 +116,28 @@
     in_specs = [column(col) for col in piece_cols]
     in_specs += [
         pl.BlockSpec((rows, BLK), lambda h: (0, q * ratio + h)),
-        pl.BlockSpec((1, depth, BLK), lambda h: (h, 0, 0)),
+        pl.BlockSpec((1, depth, BLK), lambda h: (at * ratio + h, 0, 0)),
     ]
     args = list(piece_arrays) + [cot, w]
     aliases = {}
-    if hidden_prev is not None:
-        aliases = {len(args): 0}
-        args.append(hidden_prev)
-        in_specs.append(pl.BlockSpec(memory_space=pl.ANY))
+    for output, previous in enumerate((hidden_prev, dw_prev)):
+        if previous is not None:
+            aliases[len(args)] = output
+            args.append(previous)
+            in_specs.append(pl.BlockSpec(memory_space=pl.ANY))
     whole = lambda cols: pl.BlockSpec((rows, cols), lambda h: (0, 0))
     out_specs = [
         pl.BlockSpec((rows, BLK), lambda h: (0, q * ratio + h)),
-        pl.BlockSpec((1, depth, BLK), lambda h: (h, 0, 0)),
+        pl.BlockSpec((1, depth, BLK), lambda h: (at * ratio + h, 0, 0)),
         whole(local * BLK),
     ] + [whole(BLK)] * (n_far + 1)
     out_shape = [
         jax.ShapeDtypeStruct((rows, wide), BF16),
-        jax.ShapeDtypeStruct((ratio, depth, BLK), BF16),
+        jax.ShapeDtypeStruct(w.shape, BF16),
         jax.ShapeDtypeStruct((rows, local * BLK), F32),
     ] + [jax.ShapeDtypeStruct((rows, BLK), BF16)] * n_far + [jax.ShapeDtypeStruct((rows, BLK), F32)]
     return pl.pallas_call(
-        functools.partial(chunk_kernel, factors, local, hidden_prev is not None),
+        functools.partial(chunk_kernel, factors, local, len(aliases)),
         grid=(ratio,),
         in_specs=in_specs,
         out_specs=out_specs,
@@ -154,33 +182,35 @@
     far_masks = [(1 << b) // blocks for b in range(LOG) if 1 << b >= blocks]
     n_far = len(far_masks)
     factors = LOG + 2
+    chips = lax.axis_size("dp") // 2
 
     right_blocks = right_factor.reshape(share, hidden_blocks, BLK).transpose(1, 0, 2)
     weights = []
-    for q in range(blocks):
-        part = slice(q * ratio, (q + 1) * ratio)
+    span = max(1, blocks // 2)
+    for first in range(0, blocks, span):
+        part = slice(first * ratio, (first + span) * ratio)
         local_w = jnp.concatenate([butterfly[part], right_blocks[part][:, None]], axis=1)
         full = lax.all_gather(local_w, "dp", axis=2, tiled=True)
-        weights.append(full.reshape(ratio, factors * BLK, BLK))
+        weights.append(full.reshape(span * ratio, factors * BLK, BLK))
 
     left_full = lax.all_gather(left_factor, "dp", axis=0, tiled=True)
     far_tokens = [swapped(tokens, "tensor", mask) for mask in far_masks]
     low_part = jnp.dot(tokens, left_full, preferred_element_type=F32).astype(BF16)
     low = summed_over(low_part, "tensor")
 
-    hidden = None
+    hidden = dw = None
     locs, fars, low_back, grads = [], [[] for _ in far_masks], None, []
     for q in range(blocks):
+        at = q % span
         arrays = [tokens] * len(local_masks) + far_tokens + [low]
         columns = [q ^ mask for mask in local_masks] + [q] * n_far + [0]
         hidden, dw, loc, *more = run_chunk(
-            q, ratio, len(local_masks), arrays, columns, cotangent, weights[q], hidden
+            q, at, ratio, len(local_masks), arrays, columns, cotangent, weights[q // span],
+            hidden, dw if at else None,
         )
-        grads.append(
-            lax.psum_scatter(
-                dw.reshape(ratio, factors, BLK, BLK), "dp", scatter_dimension=2, tiled=True
-            )
-        )
+        if at == span - 1:
+            blocks_dw = dw.reshape(span * ratio, factors, BLK, BLK)
+            grads.append(lax.psum_scatter(blocks_dw, "dp", scatter_dimension=2, tiled=True))
         locs.append(loc)
         for i, mask in enumerate(far_masks):
             fars[i].append(swapped(more[i], "tensor", mask))
@@ -188,7 +218,15 @@
 
     grad_low = summed_over(low_back.astype(BF16), "tensor")
     grad_first = jnp.einsum("td,tr->dr", tokens, grad_low, preferred_element_type=F32)
-    sum_first = lax.psum_scatter(grad_first.astype(BF16), "dp", scatter_dimension=0, tiled=True)
+    grad_first = grad_first.astype(BF16)
+    if chips <= 4:
+        by_owner = grad_first.reshape(chips, 2, -1, BLK)
+        core = lax.axis_index("dp") % 2
+        mine = lax.dynamic_index_in_dim(by_owner, core, 1, keepdims=False)
+        theirs = lax.dynamic_index_in_dim(by_owner, 1 - core, 1, keepdims=False)
+        sum_first = line_scatter(mine, theirs)
+    else:
+        sum_first = lax.psum_scatter(grad_first, "dp", scatter_dimension=0, tiled=True)
     grad_tokens = pl.pallas_call(
         functools.partial(final_kernel, blocks, local_masks, n_far),
         out_shape=jax.ShapeDtypeStruct(tokens.shape, BF16),

time: 377 us -> 300 us (0.80)
  waiting for transfers between devices: 219 us -> 141 us
  local copies, waits for them, and re-layouts: 40.6 us -> 30.1 us
  starting transfers between devices: 22.2 us -> 31.7 us
    reduce_scatter x4 -> x2, waiting for transfers between devices: 97.1 us -> 39.5 us  [per_device(): lax.psum_scatter(blocks_dw, 'dp', scatter_dimension=2, tiled=True)]
    unnamed x10 -> x4, waiting for transfers between devices: 30.1 us -> 0.07 us
    unnamed x63 -> x59, local copies, waits for them, and re-layouts: 36.2 us -> 22 us
    ppermute x0 -> x6, starting transfers between devices: none -> 10.9 us  [moved(): return lax.ppermute(x, 'dp', pairs)]
    convert_element_type x0 -> x5, other arithmetic: none -> 4.96 us  [the longest x2 1.56 us: line_scatter(): right = moved(going_right.astype(BF16), 1, range(0, step))]
    ppermute x16 -> x17, waiting for transfers between devices: 34 us -> 37.5 us  [swapped(): return lax.ppermute(block, axis, [(i, i ^ mask) for i in range(count)])]
    all_gather x4 -> x2, waiting for transfers between devices: 57.9 us -> 61.2 us  [per_device(): full = lax.all_gather(local_w, 'dp', axis=2, tiled=True)]
    ppermute x16 -> x17, starting transfers between devices: 21.6 us -> 20.5 us  [swapped(): return lax.ppermute(block, axis, [(i, i ^ mask) for i in range(count)])]
  transfers between devices with their start and end apart: 25 -> 27, of which waited for: 18 -> 17; matrix products, arithmetic and copies ran while one was open for 4% -> 4% of each run, Pallas kernels for 15% -> 19%
where the time goes in v3:
time: 300 us; the launch traced here: 299 us
  waiting for transfers between devices  141 us (47%)
  Pallas kernels  57.1 us (19%)
  starting transfers between devices  31.7 us (11%)
  local copies, waits for them, and re-layouts  30.1 us (10%)
  blocking collectives  17.3 us (6%)
  between operations  14.1 us (5%)
  other arithmetic  7.27 us (2%)
    all_gather x2, waiting for transfers between devices, per_device(): full = lax.all_gather(local_w, 'dp', axis=2, tiled=True)  61.2 us
    pallas_call x4, Pallas kernels, run_chunk(): pl.pallas_call(functools.partial(chunk_kernel, factors, local, len(aliase...  54.3 us
    reduce_scatter x2, waiting for transfers between devices, per_device(): lax.psum_scatter(blocks_dw, 'dp', scatter_dimension=2, tiled=True)  39.5 us
    ppermute x17, waiting for transfers between devices, swapped(): return lax.ppermute(block, axis, [(i, i ^ mask) for i in range(count)])  37.5 us
    unnamed x59, local copies, waits for them, and re-layouts  22 us
    ppermute x17, starting transfers between devices, swapped(): return lax.ppermute(block, axis, [(i, i ^ mask) for i in range(count)])  20.5 us
    all_gather x1, blocking collectives, per_device(): left_full = lax.all_gather(left_factor, 'dp', axis=0, tiled=True)  17.3 us
    ppermute x6, starting transfers between devices, moved(): return lax.ppermute(x, 'dp', pairs)  10.9 us
  transfers between devices with their start and end apart: 27, of which 17 were waited for; matrix products, arithmetic and copies ran while one was open for 4% of the time, Pallas kernels for 19%

profile of v3, /device:TPU:0, one launch (start us, length us, event | category | flops | bytes accessed | tf_op | source)
XLA Modules:
  0.0 299.2 jit_solution(11376069241714941008)
XLA Ops:
  12.1 3.0 collective-permute-start.1
  15.0 1.5 collective-permute-start
  16.5 17.3 %all_gather.9.refs_13_ = bf16[1024,256]{1,0:T(8,128)(2,1)S(1)} all-gather(bf16[128,256]{1,0:T(8,128)(2,1)S(1)} %copy-done.27), channel_id=1, replica_groups=mesh['dp'=8,'tensor'=4] {'dp'}, dimensions={0}, use_global_device_ids=true | all-gather | bytes 589824 | tf_op jit(solution)/shard_map/all_gather | solution.py:196
  35.6 2.3 collective-permute-start.2
  37.8 8.3 %collective-permute-done.4 = bf16[512,256]{1,0:T(8,128)(2,1)S(1)} collective-permute-done((bf16[512,256]{1,0:T(8,128)(2,1)S(1)}, bf16[512,256]{1,0:T(8,128)(2,1)S(1)}, u32[]{:S(2)}, u32[]{:S(2)}) %collective-permute-start.4) | collective-permute-done | bytes 262176 | tf_op jit(solution)/shard_map/ppermute | solution.py:22
  46.2 3.2 %collective-permute-done.3 = bf16[512,256]{1,0:T(8,128)(2,1)S(1)} collective-permute-done((bf16[512,256]{1,0:T(8,128)(2,1)S(1)}, bf16[512,256]{1,0:T(8,128)(2,1)S(1)}, u32[]{:S(2)}, u32[]{:S(2)}) %collective-permute-start.3) | collective-permute-done | bytes 262176 | tf_op jit(solution)/shard_map/ppermute | solution.py:22
  49.4 1.5 collective-permute-done.2
  51.1 29.2 %all-gather.5.cloned.1.call-done = bf16[8,6,256,256]{3,2,1,0:T(8,128)(2,1)} async-done(((bf16[8,6,32,256]{3,2,1,0:T(8,128)(2,1)}), bf16[8,6,256,256]{3,2,1,0:T(8,128)(2,1)}) %all-gather.5.cloned.1.call-update) | async-done | bytes 6291472 | tf_op jit(solution)/shard_map/all_gather | solution.py:193
  80.3 2.2 copy-done.1
  82.4 13.4 %shard_map.92 = (bf16[512,4096]{1,0:T(8,128)(2,1)}, bf16[8,1536,256]{2,1,0:T(8,128)(2,1)}, f32[512,768]{1,0:T(8,128)S(1)}, bf16[512,256]{1,0:T(8,128)(2,1)}, bf1...) custom-call(bf16[512,1024]{1,0:T(8,128)(2,1)S(1)} %copy-done, bf16[512,1024]{1,0:T(8,128)(2,1)S(1)} %copy-done, ...), custom_call_target="tpu_custom_call" | custom-call | flops 4831838208 | bytes 12320768 | tf_op jit(solution)/shard_map/pallas_call | solution.py:139
  97.7 13.8 %shard_map.93 = (bf16[512,4096]{1,0:T(8,128)(2,1)}, bf16[8,1536,256]{2,1,0:T(8,128)(2,1)}, f32[512,768]{1,0:T(8,128)S(1)}, bf16[512,256]{1,0:T(8,128)(2,1)}, bf1...) custom-call(bf16[512,1024]{1,0:T(8,128)(2,1)S(1)} %copy-done, ...), custom_call_target="tpu_custom_call", output_to_operand_aliasing={{0}: (8, {}), {1}: (9, {})} | custom-call | flops 4831838208 | bytes 12320768 | tf_op jit(solution)/shard_map/pallas_call | solution.py:139
  113.7 32.0 %all-gather.3.cloned.1.call-done = bf16[8,6,256,256]{3,2,1,0:T(8,128)(2,1)} async-done(((bf16[8,6,32,256]{3,2,1,0:T(8,128)(2,1)}), bf16[8,6,256,256]{3,2,1,0:T(8,128)(2,1)}) %all-gather.3.cloned.1.call-update) | async-done | bytes 6291472 | tf_op jit(solution)/shard_map/all_gather | solution.py:193
  145.8 2.2 copy-done.2
  148.0 13.4 %shard_map.94 = (bf16[512,4096]{1,0:T(8,128)(2,1)}, bf16[8,1536,256]{2,1,0:T(8,128)(2,1)}, f32[512,768]{1,0:T(8,128)S(1)}, bf16[512,256]{1,0:T(8,128)(2,1)S(1)},...) custom-call(bf16[512,1024]{1,0:T(8,128)(2,1)S(1)} %copy-done, ...), custom_call_target="tpu_custom_call", output_to_operand_aliasing={{0}: (8, {})} | custom-call | flops 4831838208 | bytes 12320768 | tf_op jit(solution)/shard_map/pallas_call | solution.py:139
  163.9 13.6 %shard_map.95 = (bf16[512,4096]{1,0:T(8,128)(2,1)}, bf16[8,1536,256]{2,1,0:T(8,128)(2,1)}, f32[512,768]{1,0:T(8,128)S(1)}, bf16[512,256]{1,0:T(8,128)(2,1)S(1)},...) custom-call(bf16[512,1024]{1,0:T(8,128)(2,1)S(1)} %copy-done, ...), custom_call_target="tpu_custom_call", output_to_operand_aliasing={{0}: (8, {}), {1}: (9, {})} | custom-call | flops 4831838208 | bytes 12320768 | tf_op jit(solution)/shard_map/pallas_call | solution.py:139
  182.6 2.4 collective-permute-start.15
  186.2 6.6 %collective-permute-done.15 = bf16[512,256]{1,0:T(8,128)(2,1)S(1)} collective-permute-done((bf16[512,256]{1,0:T(8,128)(2,1)S(1)}, bf16[512,256]{1,0:T(8,128)(2,1)S(1)}, u32[]{:S(2)}, u32[]{:S(2)}) %collective-permute-start.15) | collective-permute-done | bytes 262176 | tf_op jit(solution)/shard_map/ppermute | solution.py:22
  192.8 4.9 %collective-permute-done.14 = bf16[512,256]{1,0:T(8,128)(2,1)S(1)} collective-permute-done((bf16[512,256]{1,0:T(8,128)(2,1)S(1)}, bf16[512,256]{1,0:T(8,128)(2,1)S(1)}, u32[]{:S(2)}, u32[]{:S(2)}) %collective-permute-start.14) | collective-permute-done | bytes 262176 | tf_op jit(solution)/shard_map/ppermute | solution.py:22
  206.5 2.4 collective-permute-done.17
  208.9 5.0 %collective-permute-start.18 = (bf16[128,256]{1,0:T(8,128)(2,1)S(1)}, bf16[128,256]{1,0:T(8,128)(2,1)}, u32[]{:S(2)}, u32[]{:S(2)}) collective-permute-start(bf16[128,256]{1,0:T(8,128)(2,1)S(1)} %fusion.4), channel_id=1, source_target_pairs={{0,8},{4,12},{8,16},{12,20},{1,9},{5,13},{9,17},{13,21},{2,10},{6,... | collective-permute-start | bytes 196616 | tf_op jit(solution)/shard_map/ppermute | solution.py:48
  214.0 1.5 collective-permute-start.6
  217.4 1.5 fusion.5
  220.3 3.1 %collective-permute-done.6.refs_5_ = bf16[512,256]{1,0:T(8,128)(2,1)S(1)} collective-permute-done((bf16[512,256]{1,0:T(8,128)(2,1)}, bf16[512,256]{1,0:T(8,128)(2,1)S(1)}, u32[]{:S(2)}, u32[]{:S(2)}) %collective-permute-start.6) | collective-permute-done | bytes 262176 | tf_op jit(solution)/shard_map/ppermute | solution.py:22
  223.4 1.5 collective-permute-start.8
  225.8 3.2 %collective-permute-done.5.refs_4_ = bf16[512,256]{1,0:T(8,128)(2,1)S(1)} collective-permute-done((bf16[512,256]{1,0:T(8,128)(2,1)}, bf16[512,256]{1,0:T(8,128)(2,1)S(1)}, u32[]{:S(2)}, u32[]{:S(2)}) %collective-permute-start.5) | collective-permute-done | bytes 262176 | tf_op jit(solution)/shard_map/ppermute | solution.py:22
  229.0 1.5 collective-permute-start.7
  236.2 2.7 collective-permute-done.7.refs_6_
  240.1 1.4 copy-done.8
  243.0 1.4 copy-done.12
  244.4 2.9 shard_map.96
  247.3 1.5 fusion.7
  250.1 39.5 %reduce-scatter.5.cloned.1.call-done = bf16[8,6,32,256]{3,2,1,0:T(8,128)(2,1)} async-done(((bf16[8,6,256,256]{3,2,1,0:T(8,128)(2,1)}), bf16[8,6,32,256]{3,2,1,0:T(8,128)(2,1)}) %reduce-scatter.5.cloned.1.call-update) | async-done | bytes 786448 | tf_op jit(solution)/shard_map/reduce_scatter | solution.py:213
  (113 shorter events, 45.0 us)
Async XLA Ops:
  7.2 73.1 %all-gather.5.cloned.1.call-start = ((), (), s32[]{:S(2)}) async-start(), calls=%async_computation.3 | async-start | bytes 7077888 | tf_op jit(solution)/shard_map/all_gather | solution.py:193
  10.6 135.2 %all-gather.3.cloned.1.call-start = ((), (), s32[]{:S(2)}) async-start(), calls=%async_computation.2 | async-start | bytes 7077888 | tf_op jit(solution)/shard_map/all_gather | solution.py:193
  11.6 237.2 %reduce-scatter.3.cloned.1.call-start = ((), (), s32[]{:S(2)}) async-start(), calls=%async_computation.4 | async-start | bytes 7077888 | tf_op jit(solution)/shard_map/reduce_scatter | solution.py:213
  12.1 39.0 %collective-permute-start.1 = (bf16[512,1024]{1,0:T(8,128)(2,1)S(1)}, bf16[512,1024]{1,0:T(8,128)(2,1)S(1)}, u32[]{:S(2)}, u32[]{:S(2)}) collective-permute-start(bf16[512,1024]{1,0:T(8,128)(2,1)S(1)} %copy-done), channel_id=1, source_target_pairs={{0,2},{1,3},{2,0},{3,1},{4,6},{5,7},{6,4},{7,5},{8,10},{9,11},{10,... | collective-permute-start | bytes 3145736 | tf_op jit(solution)/shard_map/ppermute | solution.py:22
  15.0 36.1 %collective-permute-start = (bf16[512,1024]{1,0:T(8,128)(2,1)S(1)}, bf16[512,1024]{1,0:T(8,128)(2,1)S(1)}, u32[]{:S(2)}, u32[]{:S(2)}) collective-permute-start(bf16[512,1024]{1,0:T(8,128)(2,1)S(1)} %copy-done), channel_id=1, source_target_pairs={{0,1},{1,0},{2,3},{3,2},{4,5},{5,4},{6,7},{7,6},{8,9},{9,8},{10,11... | collective-permute-start | bytes 3145736 | tf_op jit(solution)/shard_map/ppermute | solution.py:22
  33.8 17.2 %copy-start.3 = (bf16[1024,256]{1,0:T(8,128)(2,1)}, bf16[1024,256]{1,0:T(8,128)(2,1)S(1)}, u32[]{:S(2)}) copy-start(bf16[1024,256]{1,0:T(8,128)(2,1)S(1)} %all_gather.9.refs_13_) | copy-start | bytes 1572868
  34.3 11.9 %collective-permute-start.4 = (bf16[512,256]{1,0:T(8,128)(2,1)S(1)}, bf16[512,256]{1,0:T(8,128)(2,1)S(1)}, u32[]{:S(2)}, u32[]{:S(2)}) collective-permute-start(bf16[512,256]{1,0:T(8,128)(2,1)S(1)} %convolution_convert_fusion.1), channel_id=1, source_target_pairs={{0,3},{1,2},{2,1},{3,0},{4,7},{5,6},{6,5},{7,4},{8,11},{9,10},{10,... | collective-permute-start | bytes 786440 | tf_op jit(solution)/shard_map/ppermute | solution.py:22
  34.4 15.1 %collective-permute-start.3 = (bf16[512,256]{1,0:T(8,128)(2,1)S(1)}, bf16[512,256]{1,0:T(8,128)(2,1)S(1)}, u32[]{:S(2)}, u32[]{:S(2)}) collective-permute-start(bf16[512,256]{1,0:T(8,128)(2,1)S(1)} %convolution_convert_fusion.1), channel_id=1, source_target_pairs={{0,2},{1,3},{2,0},{3,1},{4,6},{5,7},{6,4},{7,5},{8,10},{9,11},{10,... | collective-permute-start | bytes 786440 | tf_op jit(solution)/shard_map/ppermute | solution.py:22
  35.6 15.4 %collective-permute-start.2 = (bf16[512,256]{1,0:T(8,128)(2,1)S(1)}, bf16[512,256]{1,0:T(8,128)(2,1)S(1)}, u32[]{:S(2)}, u32[]{:S(2)}) collective-permute-start(bf16[512,256]{1,0:T(8,128)(2,1)S(1)} %convolution_convert_fusion.1), channel_id=1, source_target_pairs={{0,1},{1,0},{2,3},{3,2},{4,5},{5,4},{6,7},{7,6},{8,9},{9,8},{10,11... | collective-permute-start | bytes 786440 | tf_op jit(solution)/shard_map/ppermute | solution.py:22
  97.7 13.8 %copy-start.13 = (f32[512,256]{1,0:T(8,128)}, f32[512,256]{1,0:T(8,128)S(1)}, u32[]{:S(2)}) copy-start(f32[512,256]{1,0:T(8,128)S(1)} %get-tuple-element.47) | copy-start | bytes 1572868
  113.5 176.1 %reduce-scatter.5.cloned.1.call-start = ((), (), s32[]{:S(2)}) async-start(), calls=%async_computation.5 | async-start | bytes 7077888 | tf_op jit(solution)/shard_map/reduce_scatter | solution.py:213
  182.6 10.2 %collective-permute-start.15 = (bf16[512,256]{1,0:T(8,128)(2,1)S(1)}, bf16[512,256]{1,0:T(8,128)(2,1)S(1)}, u32[]{:S(2)}, u32[]{:S(2)}) collective-permute-start(bf16[512,256]{1,0:T(8,128)(2,1)S(1)} %add_convert_fusion.1), channel_id=1, source_target_pairs={{0,3},{1,2},{2,1},{3,0},{4,7},{5,6},{6,5},{7,4},{8,11},{9,10},{10,... | collective-permute-start | bytes 786440 | tf_op jit(solution)/shard_map/ppermute | solution.py:22
  185.1 12.6 %collective-permute-start.14 = (bf16[512,256]{1,0:T(8,128)(2,1)S(1)}, bf16[512,256]{1,0:T(8,128)(2,1)S(1)}, u32[]{:S(2)}, u32[]{:S(2)}) collective-permute-start(bf16[512,256]{1,0:T(8,128)(2,1)S(1)} %add_convert_fusion.1), channel_id=1, source_target_pairs={{0,2},{1,3},{2,0},{3,1},{4,6},{5,7},{6,4},{7,5},{8,10},{9,11},{10,... | collective-permute-start | bytes 786440 | tf_op jit(solution)/shard_map/ppermute | solution.py:22
  185.6 12.1 %collective-permute-start.13 = (bf16[512,256]{1,0:T(8,128)(2,1)S(1)}, bf16[512,256]{1,0:T(8,128)(2,1)S(1)}, u32[]{:S(2)}, u32[]{:S(2)}) collective-permute-start(bf16[512,256]{1,0:T(8,128)(2,1)S(1)} %add_convert_fusion.1), channel_id=1, source_target_pairs={{0,1},{1,0},{2,3},{3,2},{4,5},{5,4},{6,7},{7,6},{8,9},{9,8},{10,11... | collective-permute-start | bytes 786440 | tf_op jit(solution)/shard_map/ppermute | solution.py:22
  199.8 40.3 %copy-start.4 = (bf16[1024,256]{1,0:T(8,128)(2,1)S(1)}, bf16[1024,256]{1,0:T(8,128)(2,1)}, u32[]{:S(2)}) copy-start(bf16[1024,256]{1,0:T(8,128)(2,1)} %copy-done.3) | copy-start | bytes 1572868
  199.8 40.3 %copy-start.6 = (f32[512,768]{1,0:T(8,128)S(1)}, f32[512,768]{1,0:T(8,128)}, u32[]{:S(2)}) copy-start(f32[512,768]{1,0:T(8,128)} %copy-done.5) | copy-start | bytes 4718596
  200.9 1.9 collective-permute-start.16
  203.8 15.8 %copy-start.26 = (bf16[4,128,256]{2,1,0:T(8,128)(2,1)}, bf16[4,128,256]{2,1,0:T(8,128)(2,1)S(1)}, u32[]{:S(2)}) copy-start(bf16[4,128,256]{2,1,0:T(8,128)(2,1)S(1)} %fusion.1) | copy-start | bytes 786436
  203.8 5.1 %collective-permute-start.17 = (bf16[128,256]{1,0:T(8,128)(2,1)S(1)}, bf16[128,256]{1,0:T(8,128)(2,1)S(1)}, u32[]{:S(2)}, u32[]{:S(2)}) collective-permute-start(bf16[128,256]{1,0:T(8,128)(2,1)S(1)} %get-tuple-element.59), channel_id=1, source_target_pairs={{0,8},{4,12},{1,9},{5,13},{2,10},{6,14},{3,11},{7,15}} | collective-permute-start | bytes 196616 | tf_op jit(solution)/shard_map/ppermute | solution.py:48
  205.2 12.3 %collective-permute-start.20 = (bf16[128,256]{1,0:T(8,128)(2,1)S(1)}, bf16[128,256]{1,0:T(8,128)(2,1)}, u32[]{:S(2)}, u32[]{:S(2)}) collective-permute-start(bf16[128,256]{1,0:T(8,128)(2,1)S(1)} %get-tuple-element.60), channel_id=1, source_target_pairs={{24,16},{28,20},{25,17},{29,21},{26,18},{30,22},{27,19},{31,23}} | collective-permute-start | bytes 196616 | tf_op jit(solution)/shard_map/ppermute | solution.py:48
  208.9 8.5 %collective-permute-start.18 = (bf16[128,256]{1,0:T(8,128)(2,1)S(1)}, bf16[128,256]{1,0:T(8,128)(2,1)}, u32[]{:S(2)}, u32[]{:S(2)}) collective-permute-start(bf16[128,256]{1,0:T(8,128)(2,1)S(1)} %fusion.4), channel_id=1, source_target_pairs={{0,8},{4,12},{8,16},{12,20},{1,9},{5,13},{9,17},{13,21},{2,10},{6,... | collective-permute-start | bytes 196616 | tf_op jit(solution)/shard_map/ppermute | solution.py:48
  214.0 9.4 %collective-permute-start.6 = (bf16[512,256]{1,0:T(8,128)(2,1)}, bf16[512,256]{1,0:T(8,128)(2,1)S(1)}, u32[]{:S(2)}, u32[]{:S(2)}) collective-permute-start(bf16[512,256]{1,0:T(8,128)(2,1)} %get-tuple-element.40), channel_id=1, source_target_pairs={{0,1},{1,0},{2,3},{3,2},{4,5},{5,4},{6,7},{7,6},{8,9},{9,8},{10,11... | collective-permute-start | bytes 786440 | tf_op jit(solution)/shard_map/ppermute | solution.py:22
  215.4 9.5 %collective-permute-start.10 = (bf16[512,256]{1,0:T(8,128)(2,1)}, bf16[512,256]{1,0:T(8,128)(2,1)S(1)}, u32[]{:S(2)}, u32[]{:S(2)}) collective-permute-start(bf16[512,256]{1,0:T(8,128)(2,1)} %get-tuple-element.44), channel_id=1, source_target_pairs={{0,2},{1,3},{2,0},{3,1},{4,6},{5,7},{6,4},{7,5},{8,10},{9,11},{10,... | collective-permute-start | bytes 786440 | tf_op jit(solution)/shard_map/ppermute | solution.py:22
  216.3 12.7 %collective-permute-start.5 = (bf16[512,256]{1,0:T(8,128)(2,1)}, bf16[512,256]{1,0:T(8,128)(2,1)S(1)}, u32[]{:S(2)}, u32[]{:S(2)}) collective-permute-start(bf16[512,256]{1,0:T(8,128)(2,1)} %get-tuple-element.39), channel_id=1, source_target_pairs={{0,1},{1,0},{2,3},{3,2},{4,5},{5,4},{6,7},{7,6},{8,9},{9,8},{10,11... | collective-permute-start | bytes 786440 | tf_op jit(solution)/shard_map/ppermute | solution.py:22
  219.0 11.5 %collective-permute-start.21 = (bf16[128,256]{1,0:T(8,128)(2,1)S(1)}, bf16[128,256]{1,0:T(8,128)(2,1)S(1)}, u32[]{:S(2)}, u32[]{:S(2)}) collective-permute-start(bf16[128,256]{1,0:T(8,128)(2,1)S(1)} %get-tuple-element.58), channel_id=1, source_target_pairs={{16,8},{20,12},{24,16},{28,20},{17,9},{21,13},{25,17},{29,21},{18,... | collective-permute-start | bytes 196616 | tf_op jit(solution)/shard_map/ppermute | solution.py:48
  219.6 12.6 %collective-permute-start.9 = (bf16[512,256]{1,0:T(8,128)(2,1)}, bf16[512,256]{1,0:T(8,128)(2,1)S(1)}, u32[]{:S(2)}, u32[]{:S(2)}) collective-permute-start(bf16[512,256]{1,0:T(8,128)(2,1)} %copy-done.21), channel_id=1, source_target_pairs={{0,2},{1,3},{2,0},{3,1},{4,6},{5,7},{6,4},{7,5},{8,10},{9,11},{10,... | collective-permute-start | bytes 786440 | tf_op jit(solution)/shard_map/ppermute | solution.py:22
  223.4 11.3 %collective-permute-start.8 = (bf16[512,256]{1,0:T(8,128)(2,1)}, bf16[512,256]{1,0:T(8,128)(2,1)}, u32[]{:S(2)}, u32[]{:S(2)}) collective-permute-start(bf16[512,256]{1,0:T(8,128)(2,1)} %copy-done.25), channel_id=1, source_target_pairs={{0,1},{1,0},{2,3},{3,2},{4,5},{5,4},{6,7},{7,6},{8,9},{9,8},{10,11... | collective-permute-start | bytes 786440 | tf_op jit(solution)/shard_map/ppermute | solution.py:22
  224.9 11.3 %collective-permute-start.12 = (bf16[512,256]{1,0:T(8,128)(2,1)}, bf16[512,256]{1,0:T(8,128)(2,1)}, u32[]{:S(2)}, u32[]{:S(2)}) collective-permute-start(bf16[512,256]{1,0:T(8,128)(2,1)} %copy-done.24), channel_id=1, source_target_pairs={{0,2},{1,3},{2,0},{3,1},{4,6},{5,7},{6,4},{7,5},{8,10},{9,11},{10,... | collective-permute-start | bytes 786440 | tf_op jit(solution)/shard_map/ppermute | solution.py:22
  229.0 9.9 %collective-permute-start.7 = (bf16[512,256]{1,0:T(8,128)(2,1)}, bf16[512,256]{1,0:T(8,128)(2,1)}, u32[]{:S(2)}, u32[]{:S(2)}) collective-permute-start(bf16[512,256]{1,0:T(8,128)(2,1)} %copy-done.23), channel_id=1, source_target_pairs={{0,1},{1,0},{2,3},{3,2},{4,5},{5,4},{6,7},{7,6},{8,9},{9,8},{10,11... | collective-permute-start | bytes 786440 | tf_op jit(solution)/shard_map/ppermute | solution.py:22
  230.5 9.6 %collective-permute-start.11 = (bf16[512,256]{1,0:T(8,128)(2,1)}, bf16[512,256]{1,0:T(8,128)(2,1)}, u32[]{:S(2)}, u32[]{:S(2)}) collective-permute-start(bf16[512,256]{1,0:T(8,128)(2,1)} %copy-done.22), channel_id=1, source_target_pairs={{0,2},{1,3},{2,0},{3,1},{4,6},{5,7},{6,4},{7,5},{8,10},{9,11},{10,... | collective-permute-start | bytes 786440 | tf_op jit(solution)/shard_map/ppermute | solution.py:22
  232.3 15.0 %collective-permute-start.19 = (bf16[128,256]{1,0:T(8,128)(2,1)}, bf16[128,256]{1,0:T(8,128)(2,1)S(1)}, u32[]{:S(2)}, u32[]{:S(2)}) collective-permute-start(bf16[128,256]{1,0:T(8,128)(2,1)} %get-tuple-element.57), channel_id=1, source_target_pairs={{0,8},{4,12},{8,16},{12,20},{16,24},{20,28},{1,9},{5,13},{9,17},{1... | collective-permute-start | bytes 196616 | tf_op jit(solution)/shard_map/ppermute | solution.py:48
  234.7 12.6 %collective-permute-start.22 = (bf16[128,256]{1,0:T(8,128)(2,1)S(1)}, bf16[128,256]{1,0:T(8,128)(2,1)}, u32[]{:S(2)}, u32[]{:S(2)}) collective-permute-start(bf16[128,256]{1,0:T(8,128)(2,1)S(1)} %fusion.3), channel_id=1, source_target_pairs={{8,0},{12,4},{16,8},{20,12},{24,16},{28,20},{9,1},{13,5},{17,9},{2... | collective-permute-start | bytes 196616 | tf_op jit(solution)/shard_map/ppermute | solution.py:48
  (23 other events, 44.7 us)
Sparse Core Ops, SparseCore 0:
  10.7 69.4 all-gather.4
  82.4 63.2 all-gather.2
  148.1 69.9 reduce-scatter.2
  220.2 69.3 reduce-scatter.4

commit v4 on v3

--- a/solution.py
+++ b/solution.py
@@ -46,6 +46,46 @@
 def moved(x, shift, sources):
     pairs = [(2 * p + c, 2 * (p + shift) + c) for p in sources for c in range(2)]
     return lax.ppermute(x, "dp", pairs)
+
+
+def line_gather(x):
+    chips = lax.axis_size("dp") // 2
+    chip = lax.axis_index("dp") // 2
+    from_left, from_right = [x], [x]
+    for step in range(1, chips):
+        from_left.append(moved(from_left[-1], 1, range(step - 1, chips - 1)))
+        from_right.append(moved(from_right[-1], -1, range(1, chips - step + 1)))
+    slots = [x] + [
+        jnp.where(chip >= j, from_left[j], from_right[chips - j]) for j in range(1, chips)
+    ]
+    own = jnp.stack(slots)
+    return own, core_swap(own)
+
+
+def rows_gather(x):
+    chips = lax.axis_size("dp") // 2
+    if chips > 4:
+        return lax.all_gather(x, "dp", axis=0, tiled=True)
+    chip, core = lax.axis_index("dp") // 2, lax.axis_index("dp") % 2
+    own, other = line_gather(x)
+    first = core == 0
+    both = jnp.stack([jnp.where(first, own, other), jnp.where(first, other, own)], axis=1)
+    slots = [
+        lax.dynamic_index_in_dim(both, (chip - s + chips) % chips, 0, keepdims=False)
+        for s in range(chips)
+    ]
+    return jnp.stack(slots).reshape((2 * chips * x.shape[0],) + x.shape[1:])
+
+
+def rows_scatter(x):
+    chips = lax.axis_size("dp") // 2
+    if chips > 4:
+        return lax.psum_scatter(x, "dp", scatter_dimension=0, tiled=True)
+    by_owner = x.reshape((chips, 2, -1) + x.shape[1:])
+    core = lax.axis_index("dp") % 2
+    mine = lax.dynamic_index_in_dim(by_owner, core, 1, keepdims=False)
+    theirs = lax.dynamic_index_in_dim(by_owner, 1 - core, 1, keepdims=False)
+    return line_scatter(mine, theirs)
 
 
 def line_scatter(mine, theirs):
@@ -68,11 +108,12 @@
 
 def chunk_kernel(factors, local, aliased, *refs):
     pieces = refs[:factors]
-    cot_ref, w_ref = refs[factors:factors + 2]
-    rest = refs[factors + 2 + aliased:]
-    hidden_ref, dw_ref, loc_ref = rest[:3]
-    far_refs = rest[3:3 + factors - 1 - local]
-    low_ref = rest[3 + factors - 1 - local]
+    cot_ref, w_ref, right_ref = refs[factors:factors + 3]
+    rest = refs[factors + 3 + aliased:]
+    hidden_ref, dw_ref, dright_ref, loc_ref = rest[:4]
+    far_refs = rest[4:4 + factors - 1 - local]
+    low_ref = rest[4 + factors - 1 - local]
+    depth = (factors - 1) * BLK
     x, xt, acc = rest[-3:]
     step = pl.program_id(0)
 
@@ -83,21 +124,25 @@
             x[:, k * BLK:(k + 1) * BLK] = piece
             xt[k * BLK:(k + 1) * BLK, :] = piece.T
 
-    w = w_ref[0]
-    preact = jnp.dot(x[...], w, preferred_element_type=F32)
+    w, right = w_ref[0], right_ref[...]
+    preact = jnp.dot(x[:, :depth], w, preferred_element_type=F32)
+    preact = preact + jnp.dot(x[:, depth:], right, preferred_element_type=F32)
     act, slope = gelu_pair(preact)
     hidden_ref[...] = act.astype(BF16)
     grad = (cot_ref[...].astype(F32) * slope).astype(BF16)
-    dw_ref[0] = jnp.dot(xt[...], grad, preferred_element_type=F32).astype(BF16)
-    back = nt_dot(grad, w)
+    dw_ref[0] = jnp.dot(xt[:depth, :], grad, preferred_element_type=F32).astype(BF16)
+    dright_ref[...] = jnp.dot(xt[depth:, :], grad, preferred_element_type=F32).astype(BF16)
+    back, low_back = nt_dot(grad, w), nt_dot(grad, right)
 
     @pl.when(step == 0)
     def _():
-        acc[...] = back
+        acc[:, :depth] = back
+        acc[:, depth:] = low_back
 
     @pl.when(step > 0)
     def _():
-        acc[...] += back
+        acc[:, :depth] += back
+        acc[:, depth:] += low_back
 
     @pl.when(step == pl.num_programs(0) - 1)
     def _():
@@ -107,7 +152,7 @@
         low_ref[...] = acc[:, (factors - 1) * BLK:]
 
 
-def run_chunk(q, at, ratio, local, piece_arrays, piece_cols, cot, w, hidden_prev, dw_prev):
+def run_chunk(q, at, ratio, local, piece_arrays, piece_cols, cot, w, right, previous):
     rows, wide = cot.shape
     factors = len(piece_arrays)
     depth = factors * BLK
@@ -116,24 +161,27 @@
     in_specs = [column(col) for col in piece_cols]
     in_specs += [
         pl.BlockSpec((rows, BLK), lambda h: (0, q * ratio + h)),
-        pl.BlockSpec((1, depth, BLK), lambda h: (at * ratio + h, 0, 0)),
+        pl.BlockSpec((1, depth - BLK, BLK), lambda h: (at * ratio + h, 0, 0)),
+        pl.BlockSpec((BLK, BLK), lambda h: (0, q * ratio + h)),
     ]
-    args = list(piece_arrays) + [cot, w]
+    args = list(piece_arrays) + [cot, w, right]
     aliases = {}
-    for output, previous in enumerate((hidden_prev, dw_prev)):
-        if previous is not None:
+    for output, array in enumerate(previous):
+        if array is not None:
             aliases[len(args)] = output
-            args.append(previous)
+            args.append(array)
             in_specs.append(pl.BlockSpec(memory_space=pl.ANY))
     whole = lambda cols: pl.BlockSpec((rows, cols), lambda h: (0, 0))
     out_specs = [
         pl.BlockSpec((rows, BLK), lambda h: (0, q * ratio + h)),
-        pl.BlockSpec((1, depth, BLK), lambda h: (at * ratio + h, 0, 0)),
+        pl.BlockSpec((1, depth - BLK, BLK), lambda h: (at * ratio + h, 0, 0)),
+        pl.BlockSpec((BLK, BLK), lambda h: (0, q * ratio + h)),
         whole(local * BLK),
     ] + [whole(BLK)] * (n_far + 1)
     out_shape = [
         jax.ShapeDtypeStruct((rows, wide), BF16),
         jax.ShapeDtypeStruct(w.shape, BF16),
+        jax.ShapeDtypeStruct(right.shape, BF16),
         jax.ShapeDtypeStruct((rows, local * BLK), F32),
     ] + [jax.ShapeDtypeStruct((rows, BLK), BF16)] * n_far + [jax.ShapeDtypeStruct((rows, BLK), F32)]
     return pl.pallas_call(
@@ -176,40 +224,38 @@
     rows = tokens.shape[0]
     blocks = tokens.shape[1] // BLK
     hidden_blocks = right_factor.shape[1] // BLK
-    share = right_factor.shape[0]
     ratio = hidden_blocks // blocks
     local_masks = [0] + [1 << b for b in range(LOG) if 1 << b < blocks]
     far_masks = [(1 << b) // blocks for b in range(LOG) if 1 << b >= blocks]
     n_far = len(far_masks)
     factors = LOG + 2
-    chips = lax.axis_size("dp") // 2
-
-    right_blocks = right_factor.reshape(share, hidden_blocks, BLK).transpose(1, 0, 2)
+
     weights = []
     span = max(1, blocks // 2)
     for first in range(0, blocks, span):
         part = slice(first * ratio, (first + span) * ratio)
-        local_w = jnp.concatenate([butterfly[part], right_blocks[part][:, None]], axis=1)
-        full = lax.all_gather(local_w, "dp", axis=2, tiled=True)
-        weights.append(full.reshape(span * ratio, factors * BLK, BLK))
+        full = lax.all_gather(butterfly[part], "dp", axis=2, tiled=True)
+        weights.append(full.reshape(span * ratio, (factors - 1) * BLK, BLK))
 
     left_full = lax.all_gather(left_factor, "dp", axis=0, tiled=True)
     far_tokens = [swapped(tokens, "tensor", mask) for mask in far_masks]
     low_part = jnp.dot(tokens, left_full, preferred_element_type=F32).astype(BF16)
     low = summed_over(low_part, "tensor")
-
-    hidden = dw = None
+    right_own, _ = lax.optimization_barrier((right_factor, low_part))
+    right_full = rows_gather(right_own)
+
+    hidden = dw = dright = None
     locs, fars, low_back, grads = [], [[] for _ in far_masks], None, []
     for q in range(blocks):
         at = q % span
         arrays = [tokens] * len(local_masks) + far_tokens + [low]
         columns = [q ^ mask for mask in local_masks] + [q] * n_far + [0]
-        hidden, dw, loc, *more = run_chunk(
+        hidden, dw, dright, loc, *more = run_chunk(
             q, at, ratio, len(local_masks), arrays, columns, cotangent, weights[q // span],
-            hidden, dw if at else None,
+            right_full, (hidden, dw if at else None, dright),
         )
         if at == span - 1:
-            blocks_dw = dw.reshape(span * ratio, factors, BLK, BLK)
+            blocks_dw = dw.reshape(span * ratio, factors - 1, BLK, BLK)
             grads.append(lax.psum_scatter(blocks_dw, "dp", scatter_dimension=2, tiled=True))
         locs.append(loc)
         for i, mask in enumerate(far_masks):
@@ -218,15 +264,8 @@
 
     grad_low = summed_over(low_back.astype(BF16), "tensor")
     grad_first = jnp.einsum("td,tr->dr", tokens, grad_low, preferred_element_type=F32)
-    grad_first = grad_first.astype(BF16)
-    if chips <= 4:
-        by_owner = grad_first.reshape(chips, 2, -1, BLK)
-        core = lax.axis_index("dp") % 2
-        mine = lax.dynamic_index_in_dim(by_owner, core, 1, keepdims=False)
-        theirs = lax.dynamic_index_in_dim(by_owner, 1 - core, 1, keepdims=False)
-        sum_first = line_scatter(mine, theirs)
-    else:
-        sum_first = lax.psum_scatter(grad_first, "dp", scatter_dimension=0, tiled=True)
+    sum_first = rows_scatter(grad_first.astype(BF16))
+    sum_second = rows_scatter(dright)
     grad_tokens = pl.pallas_call(
         functools.partial(final_kernel, blocks, local_masks, n_far),
         out_shape=jax.ShapeDtypeStruct(tokens.shape, BF16),
@@ -240,9 +279,7 @@
         compiler_params=pltpu.CompilerParams(vmem_limit_bytes=40 * 1024 * 1024),
     )(*locs, *[f for level in fars for f in level], grad_low, left_full)
 
-    grad_all = jnp.concatenate(grads, axis=0)
-    sum_weight = grad_all[:, :LOG + 1]
-    sum_second = grad_all[:, LOG + 1].transpose(1, 0, 2).reshape(share, hidden_blocks * BLK)
+    sum_weight = jnp.concatenate(grads, axis=0)
     return (hidden, grad_tokens, sum_weight, sum_first, sum_second)
 
 

time: 300 us -> 320 us (1.067)
  waiting for transfers between devices: 141 us -> 101 us
  starting transfers between devices: 31.7 us -> 61.9 us
  other arithmetic: 7.27 us -> 22.4 us
  local copies, waits for them, and re-layouts: 30.1 us -> 41.3 us
    all_gather x2, waiting for transfers between devices: 61.2 us -> 0.02 us  [per_device(): full = lax.all_gather(butterfly[part], 'dp', axis=2, tiled=True)]
    ppermute x6 -> x18, waiting for transfers between devices: 2.45 us -> 58.1 us  [moved(): return lax.ppermute(x, 'dp', pairs)]
    reduce_scatter x2, waiting for transfers between devices: 39.5 us -> 0.01 us  [per_device(): lax.psum_scatter(blocks_dw, 'dp', scatter_dimension=2, tiled=True)]
    ppermute x6 -> x18, starting transfers between devices: 10.9 us -> 43.3 us  [moved(): return lax.ppermute(x, 'dp', pairs)]
    unnamed x59 -> x81, local copies, waits for them, and re-layouts: 22 us -> 31.7 us
    ppermute x17 -> x19, waiting for transfers between devices: 37.5 us -> 42.6 us  [swapped(): return lax.ppermute(block, axis, [(i, i ^ mask) for i in range(count)])]
    convert_element_type x2 -> x4, other arithmetic: 1.56 us -> 6.26 us  [line_scatter(): right = moved(going_right.astype(BF16), 1, range(0, step))]
    ppermute x17 -> x19, starting transfers between devices: 20.5 us -> 18.3 us  [swapped(): return lax.ppermute(block, axis, [(i, i ^ mask) for i in range(count)])]
  transfers between devices with their start and end apart: 27 -> 41, of which waited for: 17 -> 13; matrix products, arithmetic and copies ran while one was open for 4% -> 9% of each run, Pallas kernels for 19% -> 18%
where the time goes in v4:
time: 320 us; the launch traced here: 319 us
  waiting for transfers between devices  101 us (32%)
  starting transfers between devices  61.9 us (19%)
  Pallas kernels  58.3 us (18%)
  local copies, waits for them, and re-layouts  41.3 us (13%)
  other arithmetic  22.4 us (7%)
  blocking collectives  17.1 us (5%)
  between operations  14.3 us (4%)
    ppermute x18, waiting for transfers between devices, moved(): return lax.ppermute(x, 'dp', pairs)  58.1 us
    pallas_call x4, Pallas kernels, run_chunk(): pl.pallas_call(functools.partial(chunk_kernel, factors, local, len(aliase...  55.5 us
    ppermute x18, starting transfers between devices, moved(): return lax.ppermute(x, 'dp', pairs)  43.3 us
    ppermute x19, waiting for transfers between devices, swapped(): return lax.ppermute(block, axis, [(i, i ^ mask) for i in range(count)])  42.6 us
    unnamed x81, local copies, waits for them, and re-layouts  31.7 us
    ppermute x19, starting transfers between devices, swapped(): return lax.ppermute(block, axis, [(i, i ^ mask) for i in range(count)])  18.3 us
    all_gather x1, blocking collectives, per_device(): left_full = lax.all_gather(left_factor, 'dp', axis=0, tiled=True)  17.1 us
  transfers between devices with their start and end apart: 41, of which 13 were waited for; matrix products, arithmetic and copies ran while one was open for 9% of the time, Pallas kernels for 18%

profile of v4, /device:TPU:0, one launch (start us, length us, event | category | flops | bytes accessed | tf_op | source)
XLA Modules:
  0.0 318.6 jit_solution(17197298127146041501)
XLA Ops:
  7.2 2.5 fusion.19
  10.6 17.1 %all_gather.9.refs_13_ = bf16[1024,256]{1,0:T(8,128)(2,1)S(1)} all-gather(bf16[128,256]{1,0:T(8,128)(2,1)S(1)} %copy-done.38), channel_id=1, replica_groups=mesh['dp'=8,'tensor'=4] {'dp'}, dimensions={0}, use_global_device_ids=true | all-gather | bytes 589824 | tf_op jit(solution)/shard_map/all_gather | solution.py:240
  30.3 4.6 %collective-permute-start.5 = (bf16[32,4096]{1,0:T(8,128)(2,1)S(1)}, bf16[32,4096]{1,0:T(8,128)(2,1)S(1)}, u32[]{:S(2)}, u32[]{:S(2)}) collective-permute-start(bf16[32,4096]{1,0:T(8,128)(2,1)S(1)} %copy-done.35), channel_id=1, source_target_pairs={{0,8},{4,12},{8,16},{12,20},{16,24},{20,28},{1,9},{5,13},{9,17},{1... | collective-permute-start | bytes 786440 | tf_op jit(solution)/shard_map/ppermute | solution.py:48
  34.8 16.4 %collective-permute-done.6 = bf16[32,4096]{1,0:T(8,128)(2,1)S(1)} collective-permute-done((bf16[32,4096]{1,0:T(8,128)(2,1)S(1)}, bf16[32,4096]{1,0:T(8,128)(2,1)S(1)}, u32[]{:S(2)}, u32[]{:S(2)}) %collective-permute-start.6) | collective-permute-done | bytes 262176 | tf_op jit(solution)/shard_map/ppermute | solution.py:48
  53.2 18.2 %collective-permute-done.7 = bf16[32,4096]{1,0:T(8,128)(2,1)S(1)} collective-permute-done((bf16[32,4096]{1,0:T(8,128)(2,1)S(1)}, bf16[32,4096]{1,0:T(8,128)(2,1)S(1)}, u32[]{:S(2)}, u32[]{:S(2)}) %collective-permute-start.7) | collective-permute-done | bytes 262176 | tf_op jit(solution)/shard_map/ppermute | solution.py:48
  73.4 11.2 %collective-permute-done.8 = bf16[32,4096]{1,0:T(8,128)(2,1)S(1)} collective-permute-done((bf16[32,4096]{1,0:T(8,128)(2,1)S(1)}, bf16[32,4096]{1,0:T(8,128)(2,1)S(1)}, u32[]{:S(2)}, u32[]{:S(2)}) %collective-permute-start.8) | collective-permute-done | bytes 262176 | tf_op jit(solution)/shard_map/ppermute | solution.py:48
  85.8 2.4 collective-permute-start.4
  90.7 5.2 %collective-permute-done.4 = bf16[512,256]{1,0:T(8,128)(2,1)} collective-permute-done((bf16[512,256]{1,0:T(8,128)(2,1)S(1)}, bf16[512,256]{1,0:T(8,128)(2,1)}, u32[]{:S(2)}, u32[]{:S(2)}) %collective-permute-start.4) | collective-permute-done | bytes 262176 | tf_op jit(solution)/shard_map/ppermute | solution.py:22
  97.4 3.8 %collective-permute-done.3 = bf16[512,256]{1,0:T(8,128)(2,1)} collective-permute-done((bf16[512,256]{1,0:T(8,128)(2,1)S(1)}, bf16[512,256]{1,0:T(8,128)(2,1)}, u32[]{:S(2)}, u32[]{:S(2)}) %collective-permute-start.3) | collective-permute-done | bytes 262176 | tf_op jit(solution)/shard_map/ppermute | solution.py:22
  103.7 19.9 %collective-permute-done.1.refs_4_ = bf16[512,1024]{1,0:T(8,128)(2,1)} collective-permute-done((bf16[512,1024]{1,0:T(8,128)(2,1)S(1)}, bf16[512,1024]{1,0:T(8,128)(2,1)}, u32[]{:S(2)}, u32[]{:S(2)}) %collective-permute-start.1) | collective-permute-done | bytes 1048608 | tf_op jit(solution)/shard_map/ppermute | solution.py:22
  124.5 2.2 copy-done.1
  128.0 13.6 %shard_map.92 = (bf16[512,4096]{1,0:T(8,128)(2,1)}, bf16[8,1280,256]{2,1,0:T(8,128)(2,1)}, bf16[256,4096]{1,0:T(8,128)(2,1)S(1)}, f32[512,768]{1,0:T(8,128)S(1)}...) custom-call(bf16[512,1024]{1,0:T(8,128)(2,1)S(1)} %copy-done, ...), custom_call_target="tpu_custom_call" | custom-call | flops 4831838208 | bytes 12320768 | tf_op jit(solution)/shard_map/pallas_call | solution.py:187
  143.1 14.2 %shard_map.93 = (bf16[512,4096]{1,0:T(8,128)(2,1)}, bf16[8,1280,256]{2,1,0:T(8,128)(2,1)}, bf16[256,4096]{1,0:T(8,128)(2,1)S(1)}, f32[512,768]{1,0:T(8,128)S(1)}...) custom-call(bf16[512,1024]{1,0:T(8,128)(2,1)S(1)} %copy-done, ...), custom_call_target="tpu_custom_call", output_to_operand_aliasing={{0}: (9, {}), {1}: (10, {}), {2}: (11, {})} | custom-call | flops 4831838208 | bytes 12320768 | tf_op jit(solution)/shard_map/pallas_call | solution.py:187
  160.9 2.2 copy-done.2
  165.9 13.8 %shard_map.94 = (bf16[512,4096]{1,0:T(8,128)(2,1)}, bf16[8,1280,256]{2,1,0:T(8,128)(2,1)}, bf16[256,4096]{1,0:T(8,128)(2,1)S(1)}, f32[512,768]{1,0:T(8,128)S(1)}...) custom-call(bf16[512,1024]{1,0:T(8,128)(2,1)S(1)} %copy-done, ...), custom_call_target="tpu_custom_call", output_to_operand_aliasing={{0}: (9, {}), {2}: (10, {})} | custom-call | flops 4831838208 | bytes 12320768 | tf_op jit(solution)/shard_map/pallas_call | solution.py:187
  181.9 14.0 %shard_map.95 = (bf16[512,4096]{1,0:T(8,128)(2,1)}, bf16[8,1280,256]{2,1,0:T(8,128)(2,1)}, bf16[256,4096]{1,0:T(8,128)(2,1)S(1)}, f32[512,768]{1,0:T(8,128)S(1)}...) custom-call(bf16[512,1024]{1,0:T(8,128)(2,1)S(1)} %copy-done, ...), custom_call_target="tpu_custom_call", output_to_operand_aliasing={{0}: (9, {}), {1}: (10, {}), {2}: (11, {})} | custom-call | flops 4831838208 | bytes 12320768 | tf_op jit(solution)/shard_map/pallas_call | solution.py:187
  200.7 1.8 add_convert_fusion.1
  207.1 5.6 %collective-permute-done.22 = bf16[512,256]{1,0:T(8,128)(2,1)S(1)} collective-permute-done((bf16[512,256]{1,0:T(8,128)(2,1)S(1)}, bf16[512,256]{1,0:T(8,128)(2,1)S(1)}, u32[]{:S(2)}, u32[]{:S(2)}) %collective-permute-start.22) | collective-permute-done | bytes 262176 | tf_op jit(solution)/shard_map/ppermute | solution.py:22
  212.6 4.5 %collective-permute-done.21 = bf16[512,256]{1,0:T(8,128)(2,1)S(1)} collective-permute-done((bf16[512,256]{1,0:T(8,128)(2,1)S(1)}, bf16[512,256]{1,0:T(8,128)(2,1)S(1)}, u32[]{:S(2)}, u32[]{:S(2)}) %collective-permute-start.21) | collective-permute-done | bytes 262176 | tf_op jit(solution)/shard_map/ppermute | solution.py:22
  220.0 1.9 constant_dynamic-slice_fusion.1
  234.2 2.8 collective-permute-start.25
  237.7 7.2 %collective-permute-done.31 = bf16[32,4096]{1,0:T(8,128)(2,1)S(1)} collective-permute-done((bf16[32,4096]{1,0:T(8,128)(2,1)S(1)}, bf16[32,4096]{1,0:T(8,128)(2,1)S(1)}, u32[]{:S(2)}, u32[]{:S(2)}) %collective-permute-start.31) | collective-permute-done | bytes 262176 | tf_op jit(solution)/shard_map/ppermute | solution.py:48
  246.6 5.1 %collective-permute-start.32 = (bf16[32,4096]{1,0:T(8,128)(2,1)}, bf16[32,4096]{1,0:T(8,128)(2,1)}, u32[]{:S(2)}, u32[]{:S(2)}) collective-permute-start(bf16[32,4096]{1,0:T(8,128)(2,1)} %fusion.8), channel_id=1, source_target_pairs={{0,8},{4,12},{8,16},{12,20},{1,9},{5,13},{9,17},{13,21},{2,10},{6,... | collective-permute-start | bytes 786440 | tf_op jit(solution)/shard_map/ppermute | solution.py:48
  258.1 5.2 %collective-permute-done.32 = bf16[32,4096]{1,0:T(8,128)(2,1)} collective-permute-done((bf16[32,4096]{1,0:T(8,128)(2,1)}, bf16[32,4096]{1,0:T(8,128)(2,1)}, u32[]{:S(2)}, u32[]{:S(2)}) %collective-permute-start.32) | collective-permute-done | bytes 262176 | tf_op jit(solution)/shard_map/ppermute | solution.py:48
  263.9 2.1 fusion.9
  272.4 2.1 collective-permute-done.15.refs_7_
  274.5 6.8 %collective-permute-start.26 = (bf16[128,256]{1,0:T(8,128)(2,1)}, bf16[128,256]{1,0:T(8,128)(2,1)S(1)}, u32[]{:S(2)}, u32[]{:S(2)}) collective-permute-start(bf16[128,256]{1,0:T(8,128)(2,1)} %get-tuple-element.77), channel_id=1, source_target_pairs={{0,8},{4,12},{8,16},{12,20},{16,24},{20,28},{1,9},{5,13},{9,17},{1... | collective-permute-start | bytes 196616 | tf_op jit(solution)/shard_map/ppermute | solution.py:48
  282.7 1.8 fusion.7
  285.2 10.1 %collective-permute-start.33 = (bf16[32,4096]{1,0:T(8,128)(2,1)}, bf16[32,4096]{1,0:T(8,128)(2,1)}, u32[]{:S(2)}, u32[]{:S(2)}) collective-permute-start(bf16[32,4096]{1,0:T(8,128)(2,1)} %get-tuple-element.71), channel_id=1, source_target_pairs={{0,8},{4,12},{8,16},{12,20},{16,24},{20,28},{1,9},{5,13},{9,17},{1... | collective-permute-start | bytes 786440 | tf_op jit(solution)/shard_map/ppermute | solution.py:48
  303.4 2.7 shard_map.96
  307.7 1.9 fusion.11
  309.6 2.5 pad_maximum_fusion.1
  (172 shorter events, 79.2 us)
Async XLA Ops:
  7.2 117.4 %all-gather.5.cloned.1.call-start = ((), (), s32[]{:S(2)}) async-start(), calls=%async_computation.3 | async-start | bytes 5898240 | tf_op jit(solution)/shard_map/all_gather | solution.py:237
  9.8 151.1 %all-gather.3.cloned.1.call-start = ((), (), s32[]{:S(2)}) async-start(), calls=%async_computation.2 | async-start | bytes 5898240 | tf_op jit(solution)/shard_map/all_gather | solution.py:237
  10.5 299.0 %reduce-scatter.3.cloned.1.call-start = ((), (), s32[]{:S(2)}) async-start(), calls=%async_computation.4 | async-start | bytes 5898240 | tf_op jit(solution)/shard_map/reduce_scatter | solution.py:259
  29.0 22.2 %collective-permute-start.6 = (bf16[32,4096]{1,0:T(8,128)(2,1)S(1)}, bf16[32,4096]{1,0:T(8,128)(2,1)S(1)}, u32[]{:S(2)}, u32[]{:S(2)}) collective-permute-start(bf16[32,4096]{1,0:T(8,128)(2,1)S(1)} %copy-done.35), channel_id=1, source_target_pairs={{8,0},{12,4},{16,8},{20,12},{24,16},{28,20},{9,1},{13,5},{17,9},{2... | collective-permute-start | bytes 786440 | tf_op jit(solution)/shard_map/ppermute | solution.py:48
  30.3 22.2 %collective-permute-start.5 = (bf16[32,4096]{1,0:T(8,128)(2,1)S(1)}, bf16[32,4096]{1,0:T(8,128)(2,1)S(1)}, u32[]{:S(2)}, u32[]{:S(2)}) collective-permute-start(bf16[32,4096]{1,0:T(8,128)(2,1)S(1)} %copy-done.35), channel_id=1, source_target_pairs={{0,8},{4,12},{8,16},{12,20},{16,24},{20,28},{1,9},{5,13},{9,17},{1... | collective-permute-start | bytes 786440 | tf_op jit(solution)/shard_map/ppermute | solution.py:48
  51.2 20.2 %collective-permute-start.7 = (bf16[32,4096]{1,0:T(8,128)(2,1)S(1)}, bf16[32,4096]{1,0:T(8,128)(2,1)S(1)}, u32[]{:S(2)}, u32[]{:S(2)}) collective-permute-start(bf16[32,4096]{1,0:T(8,128)(2,1)S(1)} %collective-permute-done.6), channel_id=1, source_target_pairs={{8,0},{12,4},{16,8},{20,12},{9,1},{13,5},{17,9},{21,13},{10,2},{14... | collective-permute-start | bytes 786440 | tf_op jit(solution)/shard_map/ppermute | solution.py:48
  52.5 20.2 %collective-permute-start.9 = (bf16[32,4096]{1,0:T(8,128)(2,1)S(1)}, bf16[32,4096]{1,0:T(8,128)(2,1)S(1)}, u32[]{:S(2)}, u32[]{:S(2)}) collective-permute-start(bf16[32,4096]{1,0:T(8,128)(2,1)S(1)} %collective-permute-done.5), channel_id=1, source_target_pairs={{8,16},{12,20},{16,24},{20,28},{9,17},{13,21},{17,25},{21,29},{10,... | collective-permute-start | bytes 786440 | tf_op jit(solution)/shard_map/ppermute | solution.py:48
  71.3 13.2 %collective-permute-start.8 = (bf16[32,4096]{1,0:T(8,128)(2,1)S(1)}, bf16[32,4096]{1,0:T(8,128)(2,1)S(1)}, u32[]{:S(2)}, u32[]{:S(2)}) collective-permute-start(bf16[32,4096]{1,0:T(8,128)(2,1)S(1)} %collective-permute-done.7), channel_id=1, source_target_pairs={{8,0},{12,4},{9,1},{13,5},{10,2},{14,6},{11,3},{15,7}} | collective-permute-start | bytes 786440 | tf_op jit(solution)/shard_map/ppermute | solution.py:48
  85.8 17.1 %collective-permute-start.11 = (bf16[4,32,4096]{2,1,0:T(8,128)(2,1)}, bf16[4,32,4096]{2,1,0:T(8,128)(2,1)S(1)}, u32[]{:S(2)}, u32[]{:S(2)}) collective-permute-start(bf16[4,32,4096]{2,1,0:T(8,128)(2,1)} %pad_maximum_fusion.2), channel_id=1, source_target_pairs={{0,4},{4,0},{8,12},{12,8},{16,20},{20,16},{24,28},{28,24},{1,5},{5... | collective-permute-start | bytes 3145736 | tf_op jit(solution)/shard_map/ppermute | solution.py:22
  88.1 13.0 %collective-permute-start.3 = (bf16[512,256]{1,0:T(8,128)(2,1)S(1)}, bf16[512,256]{1,0:T(8,128)(2,1)}, u32[]{:S(2)}, u32[]{:S(2)}) collective-permute-start(bf16[512,256]{1,0:T(8,128)(2,1)S(1)} %convolution_convert_fusion.1), channel_id=1, source_target_pairs={{0,2},{1,3},{2,0},{3,1},{4,6},{5,7},{6,4},{7,5},{8,10},{9,11},{10,... | collective-permute-start | bytes 786440 | tf_op jit(solution)/shard_map/ppermute | solution.py:22
  88.7 12.8 %collective-permute-start.2 = (bf16[512,256]{1,0:T(8,128)(2,1)S(1)}, bf16[512,256]{1,0:T(8,128)(2,1)}, u32[]{:S(2)}, u32[]{:S(2)}) collective-permute-start(bf16[512,256]{1,0:T(8,128)(2,1)S(1)} %convolution_convert_fusion.1), channel_id=1, source_target_pairs={{0,1},{1,0},{2,3},{3,2},{4,5},{5,4},{6,7},{7,6},{8,9},{9,8},{10,11... | collective-permute-start | bytes 786440 | tf_op jit(solution)/shard_map/ppermute | solution.py:22
  89.3 34.3 %collective-permute-start.1 = (bf16[512,1024]{1,0:T(8,128)(2,1)S(1)}, bf16[512,1024]{1,0:T(8,128)(2,1)}, u32[]{:S(2)}, u32[]{:S(2)}) collective-permute-start(bf16[512,1024]{1,0:T(8,128)(2,1)S(1)} %copy-done), channel_id=1, source_target_pairs={{0,2},{1,3},{2,0},{3,1},{4,6},{5,7},{6,4},{7,5},{8,10},{9,11},{10,... | collective-permute-start | bytes 3145736 | tf_op jit(solution)/shard_map/ppermute | solution.py:22
  95.9 27.7 %collective-permute-start = (bf16[512,1024]{1,0:T(8,128)(2,1)S(1)}, bf16[512,1024]{1,0:T(8,128)(2,1)S(1)}, u32[]{:S(2)}, u32[]{:S(2)}) collective-permute-start(bf16[512,1024]{1,0:T(8,128)(2,1)S(1)} %copy-done), channel_id=1, source_target_pairs={{0,1},{1,0},{2,3},{3,2},{4,5},{5,4},{6,7},{7,6},{8,9},{9,8},{10,11... | collective-permute-start | bytes 3145736 | tf_op jit(solution)/shard_map/ppermute | solution.py:22
  160.6 148.9 %reduce-scatter.5.cloned.1.call-start = ((), (), s32[]{:S(2)}) async-start(), calls=%async_computation.5 | async-start | bytes 5898240 | tf_op jit(solution)/shard_map/reduce_scatter | solution.py:259
  204.1 13.1 %collective-permute-start.21 = (bf16[512,256]{1,0:T(8,128)(2,1)S(1)}, bf16[512,256]{1,0:T(8,128)(2,1)S(1)}, u32[]{:S(2)}, u32[]{:S(2)}) collective-permute-start(bf16[512,256]{1,0:T(8,128)(2,1)S(1)} %add_convert_fusion.1), channel_id=1, source_target_pairs={{0,2},{1,3},{2,0},{3,1},{4,6},{5,7},{6,4},{7,5},{8,10},{9,11},{10,... | collective-permute-start | bytes 786440 | tf_op jit(solution)/shard_map/ppermute | solution.py:22
  207.1 20.9 %collective-permute-start.30 = (bf16[4,32,4096]{2,1,0:T(8,128)(2,1)}, bf16[4,32,4096]{2,1,0:T(8,128)(2,1)}, u32[]{:S(2)}, u32[]{:S(2)}) collective-permute-start(bf16[4,32,4096]{2,1,0:T(8,128)(2,1)} %dynamic-slice_bitcast_fusion), channel_id=1, source_target_pairs={{0,4},{4,0},{8,12},{12,8},{16,20},{20,16},{24,28},{28,24},{1,5},{5... | collective-permute-start | bytes 3145736 | tf_op jit(solution)/shard_map/ppermute | solution.py:22
  231.2 13.7 %collective-permute-start.31 = (bf16[32,4096]{1,0:T(8,128)(2,1)S(1)}, bf16[32,4096]{1,0:T(8,128)(2,1)S(1)}, u32[]{:S(2)}, u32[]{:S(2)}) collective-permute-start(bf16[32,4096]{1,0:T(8,128)(2,1)S(1)} %get-tuple-element.73), channel_id=1, source_target_pairs={{0,8},{4,12},{1,9},{5,13},{2,10},{6,14},{3,11},{7,15}} | collective-permute-start | bytes 786440 | tf_op jit(solution)/shard_map/ppermute | solution.py:48
  232.7 20.5 %collective-permute-start.27 = (bf16[128,256]{1,0:T(8,128)(2,1)S(1)}, bf16[128,256]{1,0:T(8,128)(2,1)S(1)}, u32[]{:S(2)}, u32[]{:S(2)}) collective-permute-start(bf16[128,256]{1,0:T(8,128)(2,1)S(1)} %get-tuple-element.80), channel_id=1, source_target_pairs={{24,16},{28,20},{25,17},{29,21},{26,18},{30,22},{27,19},{31,23}} | collective-permute-start | bytes 196616 | tf_op jit(solution)/shard_map/ppermute | solution.py:48
  234.2 19.7 %collective-permute-start.25 = (bf16[128,256]{1,0:T(8,128)(2,1)S(1)}, bf16[128,256]{1,0:T(8,128)(2,1)S(1)}, u32[]{:S(2)}, u32[]{:S(2)}) collective-permute-start(bf16[128,256]{1,0:T(8,128)(2,1)S(1)} %fusion.15), channel_id=1, source_target_pairs={{0,8},{4,12},{8,16},{12,20},{1,9},{5,13},{9,17},{13,21},{2,10},{6,... | collective-permute-start | bytes 196616 | tf_op jit(solution)/shard_map/ppermute | solution.py:48
  237.0 19.7 %collective-permute-start.34 = (bf16[32,4096]{1,0:T(8,128)(2,1)}, bf16[32,4096]{1,0:T(8,128)(2,1)S(1)}, u32[]{:S(2)}, u32[]{:S(2)}) collective-permute-start(bf16[32,4096]{1,0:T(8,128)(2,1)} %get-tuple-element.74), channel_id=1, source_target_pairs={{24,16},{28,20},{25,17},{29,21},{26,18},{30,22},{27,19},{31,23}} | collective-permute-start | bytes 786440 | tf_op jit(solution)/shard_map/ppermute | solution.py:48
  246.6 16.6 %collective-permute-start.32 = (bf16[32,4096]{1,0:T(8,128)(2,1)}, bf16[32,4096]{1,0:T(8,128)(2,1)}, u32[]{:S(2)}, u32[]{:S(2)}) collective-permute-start(bf16[32,4096]{1,0:T(8,128)(2,1)} %fusion.8), channel_id=1, source_target_pairs={{0,8},{4,12},{8,16},{12,20},{1,9},{5,13},{9,17},{13,21},{2,10},{6,... | collective-permute-start | bytes 786440 | tf_op jit(solution)/shard_map/ppermute | solution.py:48
  251.7 14.3 %collective-permute-start.13 = (bf16[512,256]{1,0:T(8,128)(2,1)}, bf16[512,256]{1,0:T(8,128)(2,1)S(1)}, u32[]{:S(2)}, u32[]{:S(2)}) collective-permute-start(bf16[512,256]{1,0:T(8,128)(2,1)} %get-tuple-element.49), channel_id=1, source_target_pairs={{0,1},{1,0},{2,3},{3,2},{4,5},{5,4},{6,7},{7,6},{8,9},{9,8},{10,11... | collective-permute-start | bytes 786440 | tf_op jit(solution)/shard_map/ppermute | solution.py:22
  253.2 16.5 %collective-permute-start.17 = (bf16[512,256]{1,0:T(8,128)(2,1)}, bf16[512,256]{1,0:T(8,128)(2,1)S(1)}, u32[]{:S(2)}, u32[]{:S(2)}) collective-permute-start(bf16[512,256]{1,0:T(8,128)(2,1)} %get-tuple-element.53), channel_id=1, source_target_pairs={{0,2},{1,3},{2,0},{3,1},{4,6},{5,7},{6,4},{7,5},{8,10},{9,11},{10,... | collective-permute-start | bytes 786440 | tf_op jit(solution)/shard_map/ppermute | solution.py:22
  253.9 16.7 %collective-permute-start.12 = (bf16[512,256]{1,0:T(8,128)(2,1)}, bf16[512,256]{1,0:T(8,128)(2,1)S(1)}, u32[]{:S(2)}, u32[]{:S(2)}) collective-permute-start(bf16[512,256]{1,0:T(8,128)(2,1)} %get-tuple-element.48), channel_id=1, source_target_pairs={{0,1},{1,0},{2,3},{3,2},{4,5},{5,4},{6,7},{7,6},{8,9},{9,8},{10,11... | collective-permute-start | bytes 786440 | tf_op jit(solution)/shard_map/ppermute | solution.py:22
  257.5 14.3 %collective-permute-start.16 = (bf16[512,256]{1,0:T(8,128)(2,1)}, bf16[512,256]{1,0:T(8,128)(2,1)S(1)}, u32[]{:S(2)}, u32[]{:S(2)}) collective-permute-start(bf16[512,256]{1,0:T(8,128)(2,1)} %copy-done.30), channel_id=1, source_target_pairs={{0,2},{1,3},{2,0},{3,1},{4,6},{5,7},{6,4},{7,5},{8,10},{9,11},{10,... | collective-permute-start | bytes 786440 | tf_op jit(solution)/shard_map/ppermute | solution.py:22
  267.5 13.9 %collective-permute-start.35 = (bf16[32,4096]{1,0:T(8,128)(2,1)}, bf16[32,4096]{1,0:T(8,128)(2,1)}, u32[]{:S(2)}, u32[]{:S(2)}) collective-permute-start(bf16[32,4096]{1,0:T(8,128)(2,1)} %get-tuple-element.72), channel_id=1, source_target_pairs={{16,8},{20,12},{24,16},{28,20},{17,9},{21,13},{25,17},{29,21},{18,... | collective-permute-start | bytes 786440 | tf_op jit(solution)/shard_map/ppermute | solution.py:48
  269.7 14.7 %collective-permute-start.19 = (bf16[512,256]{1,0:T(8,128)(2,1)}, bf16[512,256]{1,0:T(8,128)(2,1)S(1)}, u32[]{:S(2)}, u32[]{:S(2)}) collective-permute-start(bf16[512,256]{1,0:T(8,128)(2,1)} %copy-done.31), channel_id=1, source_target_pairs={{0,2},{1,3},{2,0},{3,1},{4,6},{5,7},{6,4},{7,5},{8,10},{9,11},{10,... | collective-permute-start | bytes 786440 | tf_op jit(solution)/shard_map/ppermute | solution.py:22
  270.6 24.7 %collective-permute-start.14 = (bf16[512,256]{1,0:T(8,128)(2,1)}, bf16[512,256]{1,0:T(8,128)(2,1)S(1)}, u32[]{:S(2)}, u32[]{:S(2)}) collective-permute-start(bf16[512,256]{1,0:T(8,128)(2,1)} %copy-done.29), channel_id=1, source_target_pairs={{0,1},{1,0},{2,3},{3,2},{4,5},{5,4},{6,7},{7,6},{8,9},{9,8},{10,11... | collective-permute-start | bytes 786440 | tf_op jit(solution)/shard_map/ppermute | solution.py:22
  271.8 25.4 %collective-permute-start.18 = (bf16[512,256]{1,0:T(8,128)(2,1)}, bf16[512,256]{1,0:T(8,128)(2,1)}, u32[]{:S(2)}, u32[]{:S(2)}) collective-permute-start(bf16[512,256]{1,0:T(8,128)(2,1)} %copy-done.28), channel_id=1, source_target_pairs={{0,2},{1,3},{2,0},{3,1},{4,6},{5,7},{6,4},{7,5},{8,10},{9,11},{10,... | collective-permute-start | bytes 786440 | tf_op jit(solution)/shard_map/ppermute | solution.py:22
  274.5 31.6 %collective-permute-start.26 = (bf16[128,256]{1,0:T(8,128)(2,1)}, bf16[128,256]{1,0:T(8,128)(2,1)S(1)}, u32[]{:S(2)}, u32[]{:S(2)}) collective-permute-start(bf16[128,256]{1,0:T(8,128)(2,1)} %get-tuple-element.77), channel_id=1, source_target_pairs={{0,8},{4,12},{8,16},{12,20},{16,24},{20,28},{1,9},{5,13},{9,17},{1... | collective-permute-start | bytes 196616 | tf_op jit(solution)/shard_map/ppermute | solution.py:48
  281.4 24.8 %collective-permute-start.29 = (bf16[128,256]{1,0:T(8,128)(2,1)S(1)}, bf16[128,256]{1,0:T(8,128)(2,1)}, u32[]{:S(2)}, u32[]{:S(2)}) collective-permute-start(bf16[128,256]{1,0:T(8,128)(2,1)S(1)} %fusion.14), channel_id=1, source_target_pairs={{8,0},{12,4},{16,8},{20,12},{24,16},{28,20},{9,1},{13,5},{17,9},{2... | collective-permute-start | bytes 196616 | tf_op jit(solution)/shard_map/ppermute | solution.py:48
  285.2 22.5 %collective-permute-start.33 = (bf16[32,4096]{1,0:T(8,128)(2,1)}, bf16[32,4096]{1,0:T(8,128)(2,1)}, u32[]{:S(2)}, u32[]{:S(2)}) collective-permute-start(bf16[32,4096]{1,0:T(8,128)(2,1)} %get-tuple-element.71), channel_id=1, source_target_pairs={{0,8},{4,12},{8,16},{12,20},{16,24},{20,28},{1,9},{5,13},{9,17},{1... | collective-permute-start | bytes 786440 | tf_op jit(solution)/shard_map/ppermute | solution.py:48
  (49 other events, 379.7 us)
Sparse Core Ops, SparseCore 0:
  10.2 70.3 all-gather.4
  82.2 54.9 all-gather.2
  160.8 60.0 reduce-scatter.2
  223.0 73.9 reduce-scatter.4
